TPU v7x, 128 devices: a whole 4x4x4 slice. The times are simulated.
128 devices in a mesh: vert: 64 (over z, y_hi, x, core), row: 2 (over y_lo).
Axes of the slice: x: 4, y: 4 (y_hi: 2, y_lo: 2; y = y_hi * 2 + y_lo), z: 4, core: 2. Of those that a mesh axis runs over, the one named last changes fastest.
Arguments:
- features: float32 [524288, 256], P(('vert', 'row')), may hold values from -6 to 6
- w_self: float32 [256, 256], replicated, may hold values from -0.375 to 0.375
- w_neigh: float32 [256, 256], replicated, may hold values from -0.75 to 0.75
- bias: float32 [256], replicated, may hold values from -3 to 3
- w_head: float32 [256], replicated, may hold values from -0.75 to 0.75
- tile_weights: float32 [16384, 128, 128], P(('vert', 'row')), may hold values from 0.01 to 1
- tile_dst: int32 [16384], P(('vert', 'row')), may hold values from 0 to 31
- tile_src: int32 [16384], P(('vert', 'row')), may hold values from 0 to 167
- tile_count: int32 [128], P(('vert', 'row')), may hold values from 16 to 128, as said below
- hub_block: int32 [128], P(('vert', 'row')), may hold values from 0 to 31
- send_rows: int32 [128, 128, 8], P(('vert', 'row')), may hold values from 0 to 4095
- send_count: int32 [128, 128], P(('vert', 'row')), may hold values from 1 to 8, as said below
- labels: int32 [524288], P(('vert', 'row')), may hold values from 0 to 1
Outputs:
- grad_self: float32 [256, 256], replicated
- grad_neigh: float32 [256, 256], replicated
- grad_bias: float32 [256], replicated
- grad_head: float32 [256], replicated
Inputs may be any that keep to these rules, and one draw needn't show every extreme that they name: Tile t of a device is used when t < its tile_count; some device uses all 128 tiles and some 128 // 8. `send_count`: each sending device fills all 8 slots for at least one receiving device.
All inputs are finite; a program needn't handle non-finite values.
Results may differ from a plain program's by a relative error of at most 0.0003.
Values sent between devices are 32-bit elements; how exact they have to be, the bound alone decides.
A program may use at most 128 MiB of HBM per device.

v0:
```python
import math

import jax
import jax.numpy as jnp
from jax import lax
from jax.sharding import PartitionSpec as P

FULL_PRECISION = lax.Precision.HIGHEST


def on_device(
    features,
    w_self,
    w_neigh,
    bias,
    w_head,
    tile_weights,
    tile_dst,
    tile_src,
    tile_count,
    hub_block,
    send_rows,
    send_count,
    labels,
):
    tile_size = tile_weights.shape[1]
    tile_total = tile_weights.shape[0]
    feature_width = features.shape[1]
    block_count = features.shape[0] // tile_size
    slot_count = send_rows.shape[2]
    own_blocks = features.reshape(block_count, tile_size, feature_width)
    hub_local = lax.dynamic_slice_in_dim(own_blocks, hub_block[0], 1, 0)
    hub_blocks = lax.all_gather(hub_local, ("vert", "row"), axis=0, tiled=True)
    outgoing = features[send_rows[0]]
    slot_index = jnp.arange(slot_count, dtype=jnp.int32)
    alive = slot_index[None, :] < send_count[0][:, None]
    outgoing = jnp.where(alive[:, :, None], outgoing, jnp.zeros_like(outgoing))
    incoming = lax.all_to_all(outgoing, ("vert", "row"), split_axis=0, concat_axis=0, tiled=True)
    source_table = jnp.concatenate(
        [own_blocks, incoming.reshape(-1, tile_size, feature_width), hub_blocks], 0
    )
    active = jnp.arange(tile_total, dtype=jnp.int32) < tile_count[0]
    picked = source_table[tile_src]
    contrib = jnp.einsum("tij,tjf->tif", tile_weights, picked, precision=FULL_PRECISION)
    block_ids = jnp.arange(block_count, dtype=jnp.int32)
    selector = ((tile_dst[None, :] == block_ids[:, None]) & active[None, :]).astype(features.dtype)
    summed = jnp.einsum("bt,tif->bif", selector, contrib, precision=FULL_PRECISION)
    weight_sum = jnp.einsum(
        "bt,ti->bi", selector, jnp.sum(tile_weights, axis=2), precision=FULL_PRECISION
    )
    neigh_mean = ((own_blocks + summed) / (1.0 + weight_sum)[:, :, None]).reshape(-1, feature_width)
    pre_act = (
        jnp.dot(features, w_self, precision=FULL_PRECISION)
        + jnp.dot(neigh_mean, w_neigh, precision=FULL_PRECISION)
        + bias[None, :]
    )
    sigmoid_pre = jax.nn.sigmoid(pre_act)
    hidden = pre_act * sigmoid_pre
    head_score = jnp.dot(hidden, w_head, precision=FULL_PRECISION)
    target = 2.0 * labels.astype(features.dtype) - 1.0
    vertex_total = features.shape[0] * lax.axis_size(("vert", "row"))
    loss_scale = 1.0 / math.sqrt(vertex_total)
    dscore = (head_score - target) * loss_scale
    dpre = dscore[:, None] * w_head[None, :] * (sigmoid_pre * (1.0 + pre_act * (1.0 - sigmoid_pre)))
    local_self = jnp.dot(features.T, dpre, precision=FULL_PRECISION)
    local_neigh = jnp.dot(neigh_mean.T, dpre, precision=FULL_PRECISION)
    local_bias = jnp.sum(dpre, axis=0)
    local_head = jnp.dot(hidden.T, dscore, precision=FULL_PRECISION)
    grad_self, grad_neigh, grad_bias, grad_head = lax.psum(
        (local_self, local_neigh, local_bias, local_head), ("vert", "row")
    )
    return (grad_self, grad_neigh, grad_bias, grad_head)


def solution(mesh):
    in_specs = (
        P(("vert", "row"), None),
        P(),
        P(),
        P(),
        P(),
        P(("vert", "row"), None, None),
        P(("vert", "row")),
        P(("vert", "row")),
        P(("vert", "row")),
        P(("vert", "row")),
        P(("vert", "row"), None, None),
        P(("vert", "row"), None),
        P(("vert", "row")),
    )
    out_specs = (P(), P(), P(), P())
    return jax.shard_map(
        on_device, mesh=mesh, in_specs=in_specs, out_specs=out_specs, check_vma=False
    )
```

profile of v0, /device:TPU:1, one launch (start us, length us, event | category | flops | bytes accessed | tf_op | source)
XLA Modules:
  0.0 630.4 jit_solution(8257241849353653896)
XLA Ops:
  7.9 1.6 constant_dynamic-slice_fusion
  10.4 5.7 gather_fusion
  16.2 1.2 bitcast_select_fusion
  17.4 11.5 %all-to-all-start = ((f32[128,8,256]{2,1,0:T(8,128)}), f32[128,8,256]{2,1,0:T(8,128)S(1)}, u32[]{:S(2)}, u32[]{:S(2)}) async-start(f32[128,8,256]{2,1,0:T(8,128)} %bitcast_select_fusion), calls=%async_computation | async-start | bytes 2097152 | tf_op jit(solution)/shard_map/all_to_all | solution.py:38
  29.6 5.6 reduce_sum.18
  35.6 7.6 %fusion.21 = f32[4096,256]{1,0:T(8,128)} fusion(f32[4096,256]{1,0:T(8,128)} %param.13, f32[256,256]{1,0:T(8,128)S(1)} %copy-done), kind=kOutput, calls=%fused_computation.41 | convolution fusion | flops 3221225472 | bytes 8650752 | tf_op jit(solution)/shard_map/dot_general | solution.py:53
  43.2 8.0 %all-to-all-done = f32[128,8,256]{2,1,0:T(8,128)S(1)} async-done(((f32[128,8,256]{2,1,0:T(8,128)}), f32[128,8,256]{2,1,0:T(8,128)S(1)}, u32[]{:S(2)}, u32[]{:S(2)}) %all-to-all-start) | async-done | bytes 1048608 | tf_op jit(solution)/shard_map/all_to_all | solution.py:38
  51.2 294.8 %all-gather.2.cloned.1.call-done = f32[128,128,256]{2,1,0:T(8,128)} async-done(((f32[1,128,256]{2,1,0:T(8,128)}), f32[128,128,256]{2,1,0:T(8,128)}) %all-gather.2.cloned.1.call-update) | async-done | bytes 16777232 | tf_op jit(solution)/shard_map/all_gather | solution.py:33
  346.0 15.9 %pad_maximum_fusion = f32[168,128,256]{2,1,0:T(8,128)} fusion(f32[128,128,256]{2,1,0:T(8,128)} %all-gather.2.cloned.1.call-done, f32[8,128,256]{2,1,0:T(8,128)S(1)} %bitcast.58, f32[32,128,256]{2,1,0:T(8,128)} %bitcast.54), kind=kLoop, calls=%fused_computation.2 | loop fusion | flops 11010048 | bytes 44040192 | tf_op jit(solution)/shard_map/concatenate | solution.py:39
  362.0 17.3 %gather_fusion.1 = f32[128,128,256]{2,1,0:T(8,128)} fusion(f32[168,128,256]{2,1,0:T(8,128)} %pad_maximum_fusion, s32[1024]{0:T(1024)S(1)} %pad_clamp_fusion), kind=kCustom, calls=%fused_computation.1 | custom fusion | bytes 33554944 | tf_op jit(solution)/shard_map/gather | solution.py:43
  379.3 34.3 %convolution_bitcast_fusion = f32[128,128,256]{1,2,0:T(8,128)} fusion(f32[128,128,256]{2,1,0:T(8,128)} %gather_fusion.1, f32[128,128,128]{2,1,0:T(8,128)} %param.18), kind=kOutput, calls=%fused_computation.3 | convolution fusion | flops 6442450944 | bytes 41943040 | tf_op jit(solution)/shard_map/tij,tjf->tif/dot_general | solution.py:44
  413.6 17.7 %copy.26 = f32[128,128,256]{2,0,1:T(8,128)} copy(f32[128,128,256]{1,2,0:T(8,128)} %convolution_bitcast_fusion) | data formatting | bytes 33554432 | tf_op jit(solution)/shard_map/tij,tjf->tif/dot_general | solution.py:44
  431.2 13.7 %fusion.4 = f32[32,128,256]{2,0,1:T(8,128)S(1)} fusion(f32[32,128,256]{2,1,0:T(8,128)} %bitcast.55, f32[128,128,256]{2,0,1:T(8,128)} %copy.26, f32[32,128]{0,1:T(8,128)S(1)} %copy.28, s32[128]{0:T(128)S(1)} %copy-done.7, pred[128]{0:T(512)(128)(4,1)S(1)} %iota_compare_fusion.2), kind=kOutput, calls=%fused_computation.12 | convolution fusion | flops 1612718080 | bytes 25182848 | tf_op jit(solution)/shard_map/bt,tif->bif/dot_general | solution.py:47
  445.0 2.4 copy.29
  447.5 3.4 fusion
  450.9 4.4 fusion.5
  455.4 2.4 fusion.20
  457.9 7.5 %fusion.22 = f32[256,256]{1,0:T(8,128)} fusion(f32[4096,256]{1,0:T(8,128)S(1)} %bitcast.57, f32[4096,256]{1,0:T(8,128)S(1)} %get-tuple-element.21), kind=kOutput, calls=%fused_computation.42 | convolution fusion | flops 3221225472 | bytes 8650752 | tf_op jit(solution)/shard_map/dot_general | solution.py:66
  465.4 7.7 %convolution_bitcast_fusion.1 = f32[256,256]{0,1:T(8,128)} fusion(f32[4096,256]{1,0:T(8,128)S(1)} %get-tuple-element.21, f32[4096,256]{1,0:T(8,128)S(1)} %copy-done.2), kind=kOutput, calls=%fused_computation.20 | convolution fusion | flops 3221225472 | bytes 8650752 | tf_op jit(solution)/shard_map/dot_general | solution.py:65
  473.1 5.2 fusion.7
  478.2 67.6 %all-reduce = (f32[256]{0:T(256)}, f32[256]{0:T(256)}) all-reduce(f32[256]{0:T(256)S(1)} %get-tuple-element.20, f32[256]{0:T(256)S(1)} %bitcast.62), channel_id=1, replica_groups=mesh['vert'=64,'row'=2] {'vert','row'}, use_global_device_ids=true, to_apply=%region_4.5 | all-reduce | flops 512 | bytes 4096 | tf_op jit(solution)/shard_map/psum | solution.py:69
  545.9 74.0 %all-reduce.4.cloned.1.call-done = (f32[256,256]{0,1:T(8,128)}, f32[256,256]{1,0:T(8,128)}) async-done(((f32[256,256]{0,1:T(8,128)}, f32[256,256]{1,0:T(8,128)}), (f32[256,256]{0,1:T(8,128)}, f32[256,256]{1,0:T(8,128)})) %all-reduce.4.cloned.1.call-update) | async-done | bytes 524304 | tf_op jit(solution)/shard_map/psum | solution.py:69
  619.9 1.8 copy.30
  621.7 1.7 copy.39
  (39 shorter events, 1.5 us)
Async XLA Ops:
  7.2 28.4 %copy-start = (f32[256,256]{1,0:T(8,128)S(1)}, f32[256,256]{1,0:T(8,128)}, u32[]{:S(2)}) copy-start(f32[256,256]{1,0:T(8,128)} %param.14) | copy-start | bytes 786436
  7.2 338.9 %all-gather.2.cloned.1.call-start = ((), (), s32[]{:S(2)}) async-start(), calls=%async_computation.1 | async-start | bytes 16908288 | tf_op jit(solution)/shard_map/all_gather | solution.py:33
  10.4 5.7 copy-start.10
  17.4 33.8 %all-to-all-start = ((f32[128,8,256]{2,1,0:T(8,128)}), f32[128,8,256]{2,1,0:T(8,128)S(1)}, u32[]{:S(2)}, u32[]{:S(2)}) async-start(f32[128,8,256]{2,1,0:T(8,128)} %bitcast_select_fusion), calls=%async_computation | async-start | bytes 2097152 | tf_op jit(solution)/shard_map/all_to_all | solution.py:38
  28.9 591.0 %all-reduce.4.cloned.1.call-start = ((), (), s32[]{:S(2)}) async-start(), calls=%async_computation.2 | async-start | bytes 1048576 | tf_op jit(solution)/shard_map/psum | solution.py:69
  29.6 5.7 copy-start.7
  29.6 5.9 copy-start.11
  445.0 2.5 copy-start.4
  445.0 2.5 copy-start.5
  445.0 2.5 copy-start.8
  447.5 3.5 copy-start.9
  450.9 4.5 copy-start.3
  450.9 4.5 copy-start.6
  457.9 7.5 %copy-start.2 = (f32[4096,256]{1,0:T(8,128)S(1)}, f32[4096,256]{1,0:T(8,128)}, u32[]{:S(2)}) copy-start(f32[4096,256]{1,0:T(8,128)} %param.13) | copy-start | bytes 12582916
  473.1 150.3 %copy-start.1 = (f32[256,256]{1,0:T(8,128)S(1)}, f32[256,256]{1,0:T(8,128)}, u32[]{:S(2)}) copy-start(f32[256,256]{1,0:T(8,128)} %param.14) | copy-start | bytes 786436
Sparse Core Ops, SparseCore 0:
  10.3 335.7 all-gather.1
  473.2 146.6 all-reduce.3
where the time goes:
time: 636 us; the launch traced here: 630 us
  waiting for transfers between devices  377 us (59%)
  matrix products  83.9 us (13%)
  blocking collectives  67.6 us (11%)
  local copies, waits for them, and re-layouts  48.4 us (8%)
  other arithmetic  26 us (4%)
  between operations  15.9 us (2%)
  starting transfers between devices  11.6 us (2%)
    all_gather x1, waiting for transfers between devices, on_device(): hub_blocks = lax.all_gather(hub_local, ('vert', 'row'), axis=0, tiled=True)  295 us
    psum x1, waiting for transfers between devices, on_device(): lax.psum((local_self, local_neigh, local_bias, local_head), ('vert', 'row'))  74 us
    psum x1, blocking collectives, on_device(): lax.psum((local_self, local_neigh, local_bias, local_head), ('vert', 'row'))  67.6 us
    dot_general x1, matrix products, on_device(): jnp.einsum('tij,tjf->tif', tile_weights, picked, precision=FULL_PRECISION)  34.3 us
    dot_general x1, local copies, waits for them, and re-layouts, on_device(): jnp.einsum('tij,tjf->tif', tile_weights, picked, precision=FULL_PRECISION)  17.7 us
    gather x1, local copies, waits for them, and re-layouts, on_device(): picked = source_table[tile_src]  17.3 us
    concatenate x1, other arithmetic, on_device(): jnp.concatenate([own_blocks, incoming.reshape(-1, tile_size, feature_widt...  15.9 us
    dot_general x1, matrix products, on_device(): jnp.einsum('bt,tif->bif', selector, contrib, precision=FULL_PRECISION)  13.7 us
  transfers between devices with their start and end apart: 3, of which 3 were waited for; matrix products, arithmetic and copies ran while one was open for 4% of the time, Pallas kernels for 0%

commit v1 on v0

v1 whole, which is shorter than its diff:
```python
import functools
import math

import jax
import jax.numpy as jnp
from jax import lax
from jax.experimental import pallas as pl
from jax.experimental.pallas import tpu as pltpu
from jax.sharding import PartitionSpec as P

MESH = pl.DeviceIdType.MESH
BF16 = jnp.bfloat16
F32 = jnp.float32

PART_START = (0, 88, 176)
PART_ROWS = (88, 88, 80)
PART_HALF = (48, 40, 40)
PART_AXES = ("xyz", "yzx", "zxy")
OFFSETS = (0, 3, 1, 2)


def my_place():
    vert = lax.axis_index("vert")
    row = lax.axis_index("row")
    core = lax.rem(vert, 2)
    x = lax.rem(lax.div(vert, 2), 4)
    y = lax.rem(lax.div(vert, 8), 2) * 2 + row
    z = lax.div(vert, 16)
    return {"x": x, "y": y, "z": z}, core


def device_at(place, core):
    x, y, z = place["x"], place["y"], place["z"]
    vert = ((z * 2 + lax.div(y, 2)) * 4 + x) * 2 + core
    return (vert, lax.rem(y, 2))


def shifted(place, axis, step):
    moved = dict(place)
    moved[axis] = lax.rem(place[axis] + step, 4)
    return moved


def gather_kernel(hub_ref, table_ref, own_sem, recv1, recv2, recv3, send1, send2, send3, pair_send, pair_recv):
    place, core = my_place()
    near = {}
    for axis in "xyz":
        for step in (1, 3):
            near[axis, step] = device_at(shifted(place, axis, step), core)
    sibling = device_at(place, 1 - core)

    barrier = pltpu.get_barrier_semaphore()
    for target in list(near.values()) + [sibling]:
        pl.semaphore_signal(barrier, inc=1, device_id=target, device_id_type=MESH)
    pl.semaphore_wait(barrier, 7)

    def slot(part, where, half=None):
        start, rows = PART_START[part], PART_ROWS[part]
        if half == 0:
            rows = PART_HALF[part]
        elif half == 1:
            start, rows = start + PART_HALF[part], rows - PART_HALF[part]
        at = []
        for axis in "zyx":
            offset = where.get(axis, 0)
            at.append(pl.ds(0, 4) if offset == "all" else lax.rem(place[axis] + offset, 4))
        return table_ref.at[(core, *at, pl.ds(start, rows), slice(None))]

    def remote(src, dst, send_sem, recv_sem, target):
        return pltpu.make_async_remote_copy(
            src_ref=src, dst_ref=dst, send_sem=send_sem, recv_sem=recv_sem,
            device_id=target, device_id_type=MESH,
        )

    def send_both(part, where, axis, send_sem, recv, from_hub=False):
        dst = slot(part, where)
        src = hub_ref.at[pl.ds(PART_START[part], PART_ROWS[part]), :] if from_hub else dst
        remote(src, dst, send_sem, recv.at[0], near[axis, 1]).start()
        remote(src, dst, send_sem, recv.at[1], near[axis, 3]).start()

    def arrived(part, where, axis, sem, half=None):
        ref = slot(part, where, half)
        remote(ref, ref, sem, sem, near[axis, 1]).wait_recv()

    def pass_on(part, where, axis, send_sem, recv, half):
        ref = slot(part, where, half)
        remote(ref, ref, send_sem, recv.at[2 + half], near[axis, 1 if half == 0 else 3]).start()

    def to_sibling(part, where):
        ref = slot(part, where)
        remote(ref, ref, pair_send, pair_recv, sibling).start()

    parts = range(3)
    own = pltpu.make_async_copy(
        hub_ref, table_ref.at[core, place["z"], place["y"], place["x"]], own_sem
    )
    own.start()
    for p in parts:
        first, second, _ = PART_AXES[p]
        send_both(p, {}, first, send1.at[p], recv1.at[p], from_hub=True)
        send_both(p, {}, second, send2.at[p], recv2.at[p, 0], from_hub=True)
    own.wait()

    for side, offset in ((0, 3), (1, 1)):
        unit = OFFSETS.index(offset)
        for p in parts:
            first, second, _ = PART_AXES[p]
            where = {first: offset}
            arrived(p, where, first, recv1.at[p, side])
            pass_on(p, where, first, send1.at[p], recv1.at[p], side)
            send_both(p, where, second, send2.at[p], recv2.at[p, unit])
    for p in parts:
        first, second, third = PART_AXES[p]
        where = {first: 2}
        arrived(p, where, first, recv1.at[p, 2], 0)
        arrived(p, where, first, recv1.at[p, 3], 1)
        send_both(p, where, second, send2.at[p], recv2.at[p, 3])
        line = {first: "all"}
        send_both(p, line, third, send3.at[p], recv3.at[p, 0])
        to_sibling(p, line)

    for unit in range(4):
        for side, offset in ((0, 3), (1, 1)):
            for p in parts:
                first, second, _ = PART_AXES[p]
                where = {first: OFFSETS[unit], second: offset}
                arrived(p, where, second, recv2.at[p, unit, side])
                pass_on(p, where, second, send2.at[p], recv2.at[p, unit], side)
    for side, offset in ((0, 3), (1, 1)):
        for p in parts:
            first, second, third = PART_AXES[p]
            line = {first: "all", second: offset}
            send_both(p, line, third, send3.at[p], recv3.at[p, 1 + side])
            to_sibling(p, line)
    for p in parts:
        first, second, third = PART_AXES[p]
        for unit in range(4):
            where = {first: OFFSETS[unit], second: 2}
            arrived(p, where, second, recv2.at[p, unit, 2], 0)
            arrived(p, where, second, recv2.at[p, unit, 3], 1)
        line = {first: "all", second: 2}
        send_both(p, line, third, send3.at[p], recv3.at[p, 3])
        to_sibling(p, line)

    for unit in range(4):
        for side, offset in ((0, 3), (1, 1)):
            for p in parts:
                first, second, third = PART_AXES[p]
                line = {first: "all", second: OFFSETS[unit], third: offset}
                arrived(p, line, third, recv3.at[p, unit, side])
                pass_on(p, line, third, send3.at[p], recv3.at[p, unit], side)
                to_sibling(p, line)
    for unit in range(4):
        for p in parts:
            first, second, third = PART_AXES[p]
            line = {first: "all", second: OFFSETS[unit], third: 2}
            arrived(p, line, third, recv3.at[p, unit, 2], 0)
            arrived(p, line, third, recv3.at[p, unit, 3], 1)
            to_sibling(p, line)

    for p in parts:
        rows = pl.ds(PART_START[p], PART_ROWS[p])
        for sem, ref in (
            (send1.at[p], table_ref.at[core, 0, 0, pl.ds(0, 3), rows, :]),
            (send2.at[p], table_ref.at[core, 0, pl.ds(0, 3), pl.ds(0, 4), rows, :]),
            (send3.at[p], table_ref.at[core, pl.ds(0, 3), pl.ds(0, 4), pl.ds(0, 4), rows, :]),
        ):
            pltpu.make_async_copy(ref, ref, sem).wait()
    mine, theirs = table_ref.at[core], table_ref.at[1 - core]
    pltpu.make_async_copy(mine, mine, pair_send).wait()
    pltpu.make_async_copy(theirs, theirs, pair_recv).wait()


def gather_hubs(hub):
    dma = pltpu.SemaphoreType.DMA
    return pl.pallas_call(
        gather_kernel,
        out_shape=jax.ShapeDtypeStruct((2, 4, 4, 4, 256, 128), F32),
        in_specs=[pl.BlockSpec(memory_space=pl.ANY)],
        out_specs=pl.BlockSpec(memory_space=pl.ANY),
        scratch_shapes=[
            dma, dma((3, 4)), dma((3, 4, 4)), dma((3, 4, 4)),
            dma((3,)), dma((3,)), dma((3,)), dma, dma,
        ],
        compiler_params=pltpu.CompilerParams(collective_id=0, has_side_effects=True),
        name="gather_hubs",
    )(hub)


GROUP = 4
RING = 4
CHUNK = 256


def split(value):
    high = value.astype(BF16)
    low = (value - high.astype(F32)).astype(BF16)
    return high, low


def dot3(a, b, dims=(((1,), (0,)), ((), ()))):
    a_high, a_low = a
    b_high, b_low = b
    dot = functools.partial(lax.dot_general, dimension_numbers=dims, preferred_element_type=F32)
    return dot(a_high, b_high) + (dot(a_low, b_high) + dot(a_high, b_low))


def layer_kernel(
    loss_scale, dst_ref, src_ref, count_ref,
    feat_hbm, border_hbm, table_hbm, weights_hbm, w_self_ref, w_neigh_ref, bias_ref, head_ref, labels_ref,
    grad_self_ref, grad_neigh_ref, grad_small_ref,
    feat, weights, ring, total, weight_total, self_high, self_low, neigh_high, neigh_low,
    feat_sem, weight_sem, ring_sem,
):
    tiles = weights.shape[0]
    blocks = feat.shape[0] // 128
    border_blocks = border_hbm.shape[0]
    count = count_ref[0]
    groups = lax.div(count + (GROUP - 1), GROUP)
    load_feat = pltpu.make_async_copy(feat_hbm, feat, feat_sem)

    def load_weights(group):
        at = pl.ds(group * GROUP, GROUP)
        return pltpu.make_async_copy(weights_hbm.at[at], weights.at[at], weight_sem.at[group])

    def fetch(group):
        spot = lax.rem(group, RING)
        for k in range(GROUP):
            src = src_ref[group * GROUP + k]
            sem = ring_sem.at[spot, k]

            def halves(ref, block):
                for side in range(2):
                    pltpu.make_async_copy(
                        ref.at[block, :, pl.ds(128 * side, 128)],
                        ring.at[spot, k, pl.ds(128 * side, 128), :],
                        sem,
                    ).start()

            @pl.when(src < blocks)
            def _():
                for side in range(2):
                    pltpu.make_async_copy(
                        feat_hbm.at[pl.ds(pl.multiple_of(src * 128, 128), 128), pl.ds(128 * side, 128)],
                        ring.at[spot, k, pl.ds(128 * side, 128), :],
                        sem,
                    ).start()

            @pl.when((src >= blocks) & (src < blocks + border_blocks))
            def _():
                halves(border_hbm, src - blocks)

            @pl.when(src >= blocks + border_blocks)
            def _():
                pltpu.make_async_copy(
                    table_hbm.at[src - (blocks + border_blocks)], ring.at[spot, k], sem
                ).start()

    for group in range(RING - 1):
        @pl.when(group < groups)
        def _():
            load_weights(group).start()
            fetch(group)

    @pl.loop(RING - 1, groups)
    def _(group):
        load_weights(group).start()

    load_feat.start()
    total[...] = jnp.zeros_like(total)
    weight_total[...] = jnp.zeros_like(weight_total)
    self_high[...], self_low[...] = split(w_self_ref[...])
    neigh_high[...], neigh_low[...] = split(w_neigh_ref[...])

    @pl.loop(0, groups)
    def _(group):
        spot = lax.rem(group, RING)
        load_weights(group).wait()
        for k in range(GROUP):
            pltpu.make_async_copy(table_hbm.at[0], ring.at[spot, k], ring_sem.at[spot, k]).wait()

        @pl.when(group + (RING - 1) < groups)
        def _():
            fetch(group + (RING - 1))

        for k in range(GROUP):
            tile = group * GROUP + k
            dst = jnp.where(tile < count, dst_ref[tile], blocks)
            weight = weights[tile]
            source = jnp.concatenate([ring[spot, k, 0:128, :], ring[spot, k, 128:256, :]], axis=1)
            total[dst] += dot3(split(weight), split(source))
            weight_total[dst] += weight

    load_feat.wait()
    labels = labels_ref[...].astype(F32)
    target_columns = (2.0 * labels - 1.0).T
    lane = lax.broadcasted_iota(jnp.int32, target_columns.shape, 1)
    grad_self_ref[...] = jnp.zeros_like(grad_self_ref)
    grad_neigh_ref[...] = jnp.zeros_like(grad_neigh_ref)
    grad_small_ref[...] = jnp.zeros_like(grad_small_ref)
    per_chunk = CHUNK // 128

    @pl.loop(0, blocks // per_chunk)
    def _(chunk):
        rows = pl.ds(pl.multiple_of(chunk * CHUNK, CHUNK), CHUNK)
        own = feat[rows, :]
        at = pl.ds(chunk * per_chunk, per_chunk)
        summed = total[at].reshape(CHUNK, 256)
        weight_sum = jnp.sum(weight_total[at].reshape(CHUNK, 128), axis=1, keepdims=True)
        mean = (own + summed) * (1.0 / (1.0 + weight_sum))
        own_parts, mean_parts = split(own), split(mean)
        pre = (
            dot3(own_parts, (self_high[...], self_low[...]))
            + dot3(mean_parts, (neigh_high[...], neigh_low[...]))
            + bias_ref[...]
        )
        gate = jax.nn.sigmoid(pre)
        hidden = pre * gate
        score = jnp.sum(hidden * head_ref[...], axis=1, keepdims=True)
        target = jnp.concatenate(
            [
                jnp.sum(jnp.where(lane == chunk * per_chunk + i, target_columns, 0.0), axis=1, keepdims=True)
                for i in range(per_chunk)
            ],
            axis=0,
        )
        dscore = (score - target) * loss_scale
        dpre = dscore * head_ref[...] * (gate * (1.0 + pre * (1.0 - gate)))
        dpre_parts = split(dpre)
        by_rows = (((0,), (0,)), ((), ()))
        grad_self_ref[...] += dot3(own_parts, dpre_parts, by_rows)
        grad_neigh_ref[...] += dot3(mean_parts, dpre_parts, by_rows)
        grad_small_ref[0:1, :] += jnp.sum(dpre, axis=0, keepdims=True)
        grad_small_ref[1:2, :] += jnp.sum(hidden * dscore, axis=0, keepdims=True)


def layer(loss_scale, dst, src, count, features, border, table, weights, w_self, w_neigh, bias, head, labels):
    tiles = weights.shape[0]
    vertices, width = features.shape
    blocks = vertices // 128
    dma = pltpu.SemaphoreType.DMA
    smem = pl.BlockSpec(memory_space=pltpu.SMEM)
    vmem = pl.BlockSpec(memory_space=pltpu.VMEM)
    hbm = pl.BlockSpec(memory_space=pl.ANY)
    return pl.pallas_call(
        functools.partial(layer_kernel, loss_scale),
        out_shape=(
            jax.ShapeDtypeStruct((width, width), F32),
            jax.ShapeDtypeStruct((width, width), F32),
            jax.ShapeDtypeStruct((8, width), F32),
        ),
        in_specs=[smem] * 3 + [hbm] * 4 + [vmem] * 5,
        out_specs=(vmem, vmem, vmem),
        scratch_shapes=[
            pltpu.VMEM((vertices, width), F32),
            pltpu.VMEM((tiles, 128, 128), F32),
            pltpu.VMEM((RING, GROUP, 256, 128), F32),
            pltpu.VMEM((blocks + 1, 128, width), F32),
            pltpu.VMEM((blocks + 1, 128, 128), F32),
            pltpu.VMEM((width, width), BF16),
            pltpu.VMEM((width, width), BF16),
            pltpu.VMEM((width, width), BF16),
            pltpu.VMEM((width, width), BF16),
            dma,
            dma((tiles // GROUP,)),
            dma((RING, GROUP)),
        ],
        compiler_params=pltpu.CompilerParams(vmem_limit_bytes=48 * 2**20),
        name="layer",
    )(dst, src, count, features, border, table, weights, w_self, w_neigh, bias, head, labels)


def on_device(
    features,
    w_self,
    w_neigh,
    bias,
    w_head,
    tile_weights,
    tile_dst,
    tile_src,
    tile_count,
    hub_block,
    send_rows,
    send_count,
    labels,
):
    axes = ("vert", "row")
    width = features.shape[1]
    slots = send_rows.shape[2]
    blocks = features.shape[0] // 128
    peers = lax.axis_size(axes)

    hub = lax.dynamic_slice(features, (hub_block[0] * 128, 0), (128, width))
    hub = hub.reshape(128, 2, 128).transpose(1, 0, 2).reshape(256, 128)
    outgoing = features[send_rows[0]]
    alive = jnp.arange(slots, dtype=jnp.int32)[None, :] < send_count[0][:, None]
    outgoing = jnp.where(alive[:, :, None], outgoing, jnp.zeros_like(outgoing))
    incoming = lax.all_to_all(outgoing, axes, split_axis=0, concat_axis=0, tiled=True)
    border = incoming.reshape(-1, 128, width)
    table = gather_hubs(hub).reshape(peers, 256, 128)

    first_hub = blocks + border.shape[0]
    number = tile_src - first_hub
    y_low, core, x, y_high, z = number & 1, (number >> 1) & 1, (number >> 2) & 3, (number >> 4) & 1, number >> 5
    entry = core * 64 + z * 16 + (y_high * 2 + y_low) * 4 + x
    src = jnp.where(number < 0, tile_src, entry + first_hub)

    loss_scale = 1.0 / math.sqrt(features.shape[0] * peers)
    grad_self, grad_neigh, grad_small = layer(
        loss_scale, tile_dst, src, tile_count, features, border, table, tile_weights,
        w_self, w_neigh, bias.reshape(1, width), w_head.reshape(1, width), labels.reshape(blocks, 128),
    )
    small = grad_small[0:2].reshape(peers, 1, -1)
    small = jnp.pad(small, ((0, 0), (0, 0), (0, 128 - small.shape[2])))
    flat = jnp.concatenate(
        [grad_self.reshape(peers, -1, 128), grad_neigh.reshape(peers, -1, 128), small], axis=1
    )
    flat = lax.all_to_all(flat, axes, split_axis=0, concat_axis=0, tiled=True)
    part = jnp.sum(flat, axis=0, keepdims=True)
    flat = lax.all_to_all(
        jnp.broadcast_to(part, flat.shape), axes, split_axis=0, concat_axis=0, tiled=True
    )
    quarter = width * width // peers // 128
    grad_self = flat[:, 0:quarter].reshape(width, width)
    grad_neigh = flat[:, quarter:2 * quarter].reshape(width, width)
    small = flat[:, 2 * quarter, 0:2 * width // peers].reshape(2, width)
    return (grad_self, grad_neigh, small[0], small[1])


def solution(mesh):
    in_specs = (
        P(("vert", "row"), None),
        P(),
        P(),
        P(),
        P(),
        P(("vert", "row"), None, None),
        P(("vert", "row")),
        P(("vert", "row")),
        P(("vert", "row")),
        P(("vert", "row")),
        P(("vert", "row"), None, None),
        P(("vert", "row"), None),
        P(("vert", "row")),
    )
    out_specs = (P(), P(), P(), P())
    return jax.shard_map(
        on_device, mesh=mesh, in_specs=in_specs, out_specs=out_specs, check_vma=False
    )
```

time: 636 us -> 168 us (0.26)
  waiting for transfers between devices: 377 us -> 0.01 us
  matrix products: 83.9 us -> 0 us
  Pallas kernels: 0 us -> 78.3 us
  local copies, waits for them, and re-layouts: 48.4 us -> 11.3 us
  other arithmetic: 26 us -> 2.95 us
  between operations: 15.9 us -> 2.14 us
    all_gather x1 -> x0, waiting for transfers between devices: 295 us -> none  [on_device(): hub_blocks = lax.all_gather(hub_local, ('vert', 'row'), axis=0, tiled=True)]
    dot_general x9 -> x0, matrix products: 83.9 us -> none  [the longest x1 34.3 us: on_device(): jnp.einsum('tij,tjf->tif', tile_weights, picked, precision=FULL_PRECISION)]
    pallas_call x0 -> x2, Pallas kernels: none -> 78.3 us  [the longest x1 51.2 us: gather_hubs(): pl.pallas_call(gather_kernel, out_shape=jax.ShapeDtypeStruct((2, 4, 4, 4,...]
    psum x1 -> x0, waiting for transfers between devices: 74 us -> none  [on_device(): lax.psum((local_self, local_neigh, local_bias, local_head), ('vert', 'row'))]
    psum x1 -> x0, blocking collectives: 67.6 us -> none  [on_device(): lax.psum((local_self, local_neigh, local_bias, local_head), ('vert', 'row'))]
    all_to_all x0 -> x2, blocking collectives: none -> 61.4 us  [the longest x1 38.2 us: on_device(): flat = lax.all_to_all(flat, axes, split_axis=0, concat_axis=0, tiled=True)]
    dot_general x1 -> x0, local copies, waits for them, and re-layouts: 17.7 us -> none  [on_device(): jnp.einsum('tij,tjf->tif', tile_weights, picked, precision=FULL_PRECISION)]
    gather x1 -> x0, local copies, waits for them, and re-layouts: 17.3 us -> none  [on_device(): picked = source_table[tile_src]]
  transfers between devices with their start and end apart: 3 -> 1, of which waited for: 3 -> 0; matrix products, arithmetic and copies ran while one was open for 4% -> 1% of each run, Pallas kernels for 0% -> 31%
where the time goes in v1:
time: 168 us
  Pallas kernels  78.3 us (47%)
  blocking collectives  61.4 us (37%)
  starting transfers between devices  11.5 us (7%)
  local copies, waits for them, and re-layouts  11.3 us (7%)
  other arithmetic  2.95 us (2%)
  between operations  2.14 us (1%)
    pallas_call x1, Pallas kernels, gather_hubs(): pl.pallas_call(gather_kernel, out_shape=jax.ShapeDtypeStruct((2, 4, 4, 4,...  51.2 us
    all_to_all x1, blocking collectives, on_device(): flat = lax.all_to_all(flat, axes, split_axis=0, concat_axis=0, tiled=True)  38.2 us
    pallas_call x1, Pallas kernels, layer(): pl.pallas_call(functools.partial(layer_kernel, loss_scale), out_shape=(ja...  27.1 us
    all_to_all x1, blocking collectives, on_device(): lax.all_to_all(jnp.broadcast_to(part, flat.shape), axes, split_axis=0, co...  23.2 us
    all_to_all x1, starting transfers between devices, on_device(): lax.all_to_all(outgoing, axes, split_axis=0, concat_axis=0, tiled=True)  11.5 us
    gather x1, local copies, waits for them, and re-layouts, on_device(): outgoing = features[send_rows[0]]  5.65 us
  transfers between devices with their start and end apart: 1, of which 0 were waited for; matrix products, arithmetic and copies ran while one was open for 1% of the time, Pallas kernels for 31%

profile of v1, /device:TPU:1, one launch (start us, length us, event | category | flops | bytes accessed | tf_op | source)
XLA Modules:
  0.0 167.6 jit_solution(5449455959056486391)
XLA Ops:
  0.6 0.7 compare_select_fusion
  1.3 0.7 iota_compare_fusion
  2.1 0.1 copy.24
  2.2 0.1 reshape.117
  2.3 5.7 %gather_fusion = f32[1024,256]{1,0:T(8,128)S(1)} fusion(f32[4096,256]{1,0:T(8,128)} %feat_hbm.1, s32[1024]{0:T(1024)S(1)} %broadcast_clamp_fusion), kind=kCustom, calls=%fused_computation | custom fusion | bytes 2101248 | tf_op jit(solution)/shard_map/gather | solution.py:396
  7.9 1.2 bitcast_select_fusion
  9.1 11.5 %all-to-all-start = ((f32[128,8,256]{2,1,0:T(8,128)}), f32[128,8,256]{2,1,0:T(8,128)S(1)}, u32[]{:S(2)}, u32[]{:S(2)}) async-start(f32[128,8,256]{2,1,0:T(8,128)} %bitcast_select_fusion), calls=%async_computation | async-start | bytes 2097152 | tf_op jit(solution)/shard_map/all_to_all | solution.py:399
  21.9 0.9 constant_dynamic-slice_fusion
  22.8 0.1 copy.28
  22.9 0.8 copy.26
  23.7 51.2 %gather_hubs.1 = f32[2,4,4,4,256,128]{5,4,3,2,1,0:T(8,128)} custom-call(f32[256,128]{1,0:T(8,128)} %bitcast.23), custom_call_target="tpu_custom_call" | custom-call | tf_op jit(solution)/shard_map/gather_hubs/pallas_call | solution.py:176
  75.0 27.1 %layer.1 = (f32[256,256]{1,0:T(8,128)S(1)}, f32[256,256]{1,0:T(8,128)S(1)}, f32[8,256]{1,0:T(8,128)S(1)}) custom-call(s32[128]{0:T(128)S(1)} %copy-done.5, s32[128]{0:T(128)S(1)} %compare_select_fusion.1.src_ref, s32[1]{0:T(128)S(6)} %copy.29.count_ref, f32[4096,256]{1,0:T(8,128)} %feat_hbm.1, f32[8,128,256]{2,1,0:T(8,128)S(1)} %bitcast.18, ...), custom_call_target="tpu_custom_call" | custom-call | tf_op jit(solution)/shard_map/layer/pallas_call | solution.py:345
  102.1 0.1 reshape.110
  102.3 0.1 reshape.112
  102.4 0.1 reshape.111
  102.5 0.2 pad_maximum_fusion
  102.7 38.2 %all_to_all.15 = f32[128,9,128]{2,1,0:T(8,128)S(1)} all-to-all(f32[128,9,128]{2,1,0:T(8,128)S(1)} %pad_maximum_fusion), channel_id=1, replica_groups=mesh['vert'=64,'row'=2] {'vert','row'}, dimensions={0} | all-to-all | bytes 1179648 | tf_op jit(solution)/shard_map/all_to_all | solution.py:419
  140.9 0.1 reduce_sum.9
  141.1 23.2 %all_to_all.16 = f32[128,9,128]{2,1,0:T(8,128)S(1)} all-to-all(f32[128,9,128]{2,1,0:T(8,128)S(1)} %broadcast_in_dim.22), channel_id=1, replica_groups=mesh['vert'=64,'row'=2] {'vert','row'}, dimensions={0} | all-to-all | bytes 1179648 | tf_op jit(solution)/shard_map/all_to_all | solution.py:421
  164.4 0.8 reshape.114
  165.3 0.2 slice_reduce_fusion
  165.4 0.7 squeeze.12
  166.1 0.7 squeeze.11
  166.8 0.8 reshape.113
  (21 shorter events, 0.2 us)
Async XLA Ops:
  9.1 65.9 %all-to-all-start = ((f32[128,8,256]{2,1,0:T(8,128)}), f32[128,8,256]{2,1,0:T(8,128)S(1)}, u32[]{:S(2)}, u32[]{:S(2)}) async-start(f32[128,8,256]{2,1,0:T(8,128)} %bitcast_select_fusion), calls=%async_computation | async-start | bytes 2097152 | tf_op jit(solution)/shard_map/all_to_all | solution.py:399
  23.7 51.3 %copy-start.6 = (s32[128]{0:T(128)S(1)}, s32[128]{0:T(128)}, u32[]{:S(2)}) copy-start(s32[128]{0:T(128)} %param.20) | copy-start | bytes 1540
  23.7 51.3 %copy-start = (f32[256,256]{1,0:T(8,128)S(1)}, f32[256,256]{1,0:T(8,128)}, u32[]{:S(2)}) copy-start(f32[256,256]{1,0:T(8,128)} %w_self_ref.1) | copy-start | bytes 786436
  23.7 51.3 %copy-start.1 = (f32[256,256]{1,0:T(8,128)S(1)}, f32[256,256]{1,0:T(8,128)}, u32[]{:S(2)}) copy-start(f32[256,256]{1,0:T(8,128)} %w_neigh_ref.1) | copy-start | bytes 786436
  23.7 51.3 %copy-start.2 = (s32[4096]{0:T(1024)S(1)}, s32[4096]{0:T(1024)}, u32[]{:S(2)}) copy-start(s32[4096]{0:T(1024)} %param.25) | copy-start | bytes 49156
  23.7 51.3 %copy-start.3 = (f32[256]{0:T(256)S(1)}, f32[256]{0:T(256)}, u32[]{:S(2)}) copy-start(f32[256]{0:T(256)} %param.16) | copy-start | bytes 3076
  23.7 51.3 %copy-start.4 = (f32[256]{0:T(256)S(1)}, f32[256]{0:T(256)}, u32[]{:S(2)}) copy-start(f32[256]{0:T(256)} %param.17) | copy-start | bytes 3076
  23.7 51.3 %copy-start.5 = (s32[128]{0:T(128)S(1)}, s32[128]{0:T(128)}, u32[]{:S(2)}) copy-start(s32[128]{0:T(128)} %dst_ref.1) | copy-start | bytes 1540

commit v2 on v1

--- a/solution.py
+++ b/solution.py
@@ -208,8 +208,8 @@
 def layer_kernel(
     loss_scale, dst_ref, src_ref, count_ref,
     feat_hbm, border_hbm, table_hbm, weights_hbm, w_self_ref, w_neigh_ref, bias_ref, head_ref, labels_ref,
-    grad_self_ref, grad_neigh_ref, grad_small_ref,
-    feat, weights, ring, total, weight_total, self_high, self_low, neigh_high, neigh_low,
+    grad_ref,
+    grad_self_ref, grad_neigh_ref, grad_small_ref, feat, weights, ring, total, weight_total, self_high, self_low, neigh_high, neigh_low,
     feat_sem, weight_sem, ring_sem,
 ):
     tiles = weights.shape[0]
@@ -333,6 +333,14 @@
         grad_small_ref[0:1, :] += jnp.sum(dpre, axis=0, keepdims=True)
         grad_small_ref[1:2, :] += jnp.sum(hidden * dscore, axis=0, keepdims=True)
 
+    for i, ref in enumerate((grad_self_ref, grad_neigh_ref)):
+        for side in range(2):
+            grad_ref[pl.ds(512 * i + 256 * side, 256), :] = ref[:, 128 * side:128 * side + 128]
+    grad_ref[1024:1032, :] = jnp.zeros((8, 128), F32)
+    for i in range(4):
+        side = 128 * (i % 2)
+        grad_ref[1024 + i:1025 + i, :] = grad_small_ref[i // 2:i // 2 + 1, side:side + 128]
+
 
 def layer(loss_scale, dst, src, count, features, border, table, weights, w_self, w_neigh, bias, head, labels):
     tiles = weights.shape[0]
@@ -344,14 +352,13 @@
     hbm = pl.BlockSpec(memory_space=pl.ANY)
     return pl.pallas_call(
         functools.partial(layer_kernel, loss_scale),
-        out_shape=(
-            jax.ShapeDtypeStruct((width, width), F32),
-            jax.ShapeDtypeStruct((width, width), F32),
-            jax.ShapeDtypeStruct((8, width), F32),
-        ),
+        out_shape=jax.ShapeDtypeStruct((1032, 128), F32),
         in_specs=[smem] * 3 + [hbm] * 4 + [vmem] * 5,
-        out_specs=(vmem, vmem, vmem),
+        out_specs=vmem,
         scratch_shapes=[
+            pltpu.VMEM((width, width), F32),
+            pltpu.VMEM((width, width), F32),
+            pltpu.VMEM((8, width), F32),
             pltpu.VMEM((vertices, width), F32),
             pltpu.VMEM((tiles, 128, 128), F32),
             pltpu.VMEM((RING, GROUP, 256, 128), F32),
@@ -368,6 +375,125 @@
         compiler_params=pltpu.CompilerParams(vmem_limit_bytes=48 * 2**20),
         name="layer",
     )(dst, src, count, features, border, table, weights, w_self, w_neigh, bias, head, labels)
+
+
+def sum_kernel(
+    grad_ref, self_ref, neigh_ref, bias_ref, head_ref,
+    pair_in, plane_out, plane_in, plane_sum, z_out, z_in, whole, send_sem, recv_sem,
+):
+    place, core = my_place()
+    q = place["y"] * 4 + place["x"]
+    z = place["z"]
+    sibling = device_at(place, 1 - core)
+
+    def plane_peer(step):
+        other = lax.rem(q + step, 16)
+        return other, device_at({"x": lax.rem(other, 4), "y": lax.div(other, 4), "z": z}, core)
+
+    def z_peer(step):
+        other = lax.rem(z + step, 4)
+        return other, device_at(shifted(place, "z", step), core)
+
+    barrier = pltpu.get_barrier_semaphore()
+    targets = [sibling] + [plane_peer(s)[1] for s in range(1, 16)] + [z_peer(s)[1] for s in range(1, 4)]
+    for target in targets:
+        pl.semaphore_signal(barrier, inc=1, device_id=target, device_id_type=MESH)
+    pl.semaphore_wait(barrier, len(targets))
+
+    def send(stage, src, dst, target):
+        pltpu.make_async_remote_copy(
+            src_ref=src, dst_ref=dst, send_sem=send_sem.at[stage], recv_sem=recv_sem.at[stage],
+            device_id=target, device_id_type=MESH,
+        ).start()
+
+    def received(stage, ref):
+        pltpu.make_async_copy(ref, ref, recv_sem.at[stage]).wait()
+
+    half, other_half = core * 512, (1 - core) * 512
+    send(0, grad_ref.at[pl.ds(other_half, 512)], pair_in.at[pl.ds(0, 512)], sibling)
+    send(0, grad_ref.at[pl.ds(1024, 8)], pair_in.at[pl.ds(512, 8)], sibling)
+    received(0, pair_in)
+
+    small = grad_ref[1024:1032, :] + pair_in[512:520, :]
+    for step in range(1, 17):
+        other, target = plane_peer(step)
+        row = pl.multiple_of(other * 32, 32)
+        buffer = plane_in if step == 16 else plane_out
+        buffer[other, 0:32, :] = grad_ref[pl.ds(half + row, 32), :] + pair_in[pl.ds(row, 32), :]
+        buffer[other, 32:40, :] = small
+        if step < 16:
+            send(1, plane_out.at[other], plane_in.at[q], target)
+    received(1, plane_in.at[pl.ds(0, 15)])
+    value = plane_in[0]
+    for i in range(1, 16):
+        value = value + plane_in[i]
+    plane_sum[...] = value
+
+    for step in range(1, 5):
+        other, target = z_peer(step)
+        buffer = z_in if step == 4 else z_out
+        buffer[other, 0:8, :] = plane_sum[pl.ds(pl.multiple_of(other * 8, 8), 8), :]
+        buffer[other, 8:16, :] = plane_sum[32:40, :]
+        if step < 4:
+            send(2, z_out.at[other], z_in.at[z], target)
+    received(2, z_in.at[pl.ds(0, 3)])
+    value = (z_in[0] + z_in[1]) + (z_in[2] + z_in[3])
+
+    lot = half + q * 32
+    mine = pl.ds(pl.multiple_of(lot + z * 8, 8), 8)
+    whole[mine, :] = value[0:8]
+    for step in range(1, 4):
+        send(3, whole.at[mine], whole.at[mine], z_peer(step)[1])
+    received(3, whole.at[pl.ds(0, 24)])
+    mine = pl.ds(pl.multiple_of(lot, 32), 32)
+    for step in range(1, 16):
+        send(4, whole.at[mine], whole.at[mine], plane_peer(step)[1])
+    received(4, whole.at[pl.ds(0, 480)])
+    mine = pl.ds(pl.multiple_of(half, 512), 512)
+    send(5, whole.at[mine], whole.at[mine], sibling)
+    for i in range(4):
+        ref = (bias_ref, head_ref)[i // 2]
+        ref[0:1, 128 * (i % 2):128 * (i % 2) + 128] = value[8 + i:9 + i]
+    received(5, whole.at[pl.ds(0, 512)])
+    for i, ref in enumerate((self_ref, neigh_ref)):
+        for side in range(2):
+            ref[:, 128 * side:128 * side + 128] = whole[pl.ds(512 * i + 256 * side, 256), :]
+
+    sent = (
+        pair_in, plane_in.at[pl.ds(0, 15)], z_in.at[pl.ds(0, 3)],
+        whole.at[pl.ds(0, 24)], whole.at[pl.ds(0, 480)], whole.at[pl.ds(0, 512)],
+    )
+    for stage, ref in enumerate(sent):
+        pltpu.make_async_copy(ref, ref, send_sem.at[stage]).wait()
+
+
+def sum_grads(grads):
+    vmem = pl.BlockSpec(memory_space=pltpu.VMEM)
+    dma = pltpu.SemaphoreType.DMA
+    return pl.pallas_call(
+        sum_kernel,
+        out_shape=(
+            jax.ShapeDtypeStruct((256, 256), F32),
+            jax.ShapeDtypeStruct((256, 256), F32),
+            jax.ShapeDtypeStruct((1, 256), F32),
+            jax.ShapeDtypeStruct((1, 256), F32),
+        ),
+        in_specs=[vmem],
+        out_specs=(vmem,) * 4,
+        scratch_shapes=[
+            pltpu.VMEM((520, 128), F32),
+            pltpu.VMEM((16, 40, 128), F32),
+            pltpu.VMEM((16, 40, 128), F32),
+            pltpu.VMEM((40, 128), F32),
+            pltpu.VMEM((4, 16, 128), F32),
+            pltpu.VMEM((4, 16, 128), F32),
+            pltpu.VMEM((1024, 128), F32),
+            dma((6,)),
+            dma((6,)),
+        ],
+        compiler_params=pltpu.CompilerParams(collective_id=1, has_side_effects=True),
+        name="sum_grads",
+    )(grads)
 
 
 def on_device(
@@ -407,25 +533,12 @@
     src = jnp.where(number < 0, tile_src, entry + first_hub)
 
     loss_scale = 1.0 / math.sqrt(features.shape[0] * peers)
-    grad_self, grad_neigh, grad_small = layer(
+    grads = layer(
         loss_scale, tile_dst, src, tile_count, features, border, table, tile_weights,
         w_self, w_neigh, bias.reshape(1, width), w_head.reshape(1, width), labels.reshape(blocks, 128),
     )
-    small = grad_small[0:2].reshape(peers, 1, -1)
-    small = jnp.pad(small, ((0, 0), (0, 0), (0, 128 - small.shape[2])))
-    flat = jnp.concatenate(
-        [grad_self.reshape(peers, -1, 128), grad_neigh.reshape(peers, -1, 128), small], axis=1
-    )
-    flat = lax.all_to_all(flat, axes, split_axis=0, concat_axis=0, tiled=True)
-    part = jnp.sum(flat, axis=0, keepdims=True)
-    flat = lax.all_to_all(
-        jnp.broadcast_to(part, flat.shape), axes, split_axis=0, concat_axis=0, tiled=True
-    )
-    quarter = width * width // peers // 128
-    grad_self = flat[:, 0:quarter].reshape(width, width)
-    grad_neigh = flat[:, quarter:2 * quarter].reshape(width, width)
-    small = flat[:, 2 * quarter, 0:2 * width // peers].reshape(2, width)
-    return (grad_self, grad_neigh, small[0], small[1])
+    grad_self, grad_neigh, grad_bias, grad_head = sum_grads(grads)
+    return (grad_self, grad_neigh, grad_bias.reshape(width), grad_head.reshape(width))
 
 
 def solution(mesh):

time: 168 us -> 149 us (0.89)
  blocking collectives: 61.4 us -> 0 us
  Pallas kernels: 78.3 us -> 118 us
  local copies, waits for them, and re-layouts: 11.3 us -> 14.2 us
    all_to_all x2 -> x0, blocking collectives: 61.4 us -> none  [the longest x1 38.2 us: on_device(): flat = lax.all_to_all(flat, axes, split_axis=0, concat_axis=0, tiled=True)]
    pallas_call x1 -> x2, Pallas kernels: 27.1 us -> 66.7 us  [the longest x1 40.3 us: layer(): pl.pallas_call(functools.partial(layer_kernel, loss_scale), out_shape=jax...]
    unnamed x15 -> x21, local copies, waits for them, and re-layouts: 0.12 us -> 6.73 us
    reshape x5 -> x0, local copies, waits for them, and re-layouts: 2.03 us -> none  [the longest x1 0.84 us: on_device(): grad_neigh = flat[:, quarter:2 * quarter].reshape(width, width)]
  transfers between devices with their start and end apart: 1 -> 1, of which waited for: 0 -> 0; matrix products, arithmetic and copies ran while one was open for 1% -> 1% of each run, Pallas kernels for 31% -> 35%
where the time goes in v2:
time: 149 us; the launch traced here: 148 us
  Pallas kernels  118 us (79%)
  local copies, waits for them, and re-layouts  14.2 us (10%)
  starting transfers between devices  11.5 us (8%)
  other arithmetic  2.64 us (2%)
  between operations  2.1 us (1%)
    pallas_call x1, Pallas kernels, gather_hubs(): pl.pallas_call(gather_kernel, out_shape=jax.ShapeDtypeStruct((2, 4, 4, 4,...  51.2 us
    pallas_call x1, Pallas kernels, layer(): pl.pallas_call(functools.partial(layer_kernel, loss_scale), out_shape=jax...  40.3 us
    pallas_call x1, Pallas kernels, sum_grads(): pl.pallas_call(sum_kernel, out_shape=(jax.ShapeDtypeStruct((256, 256), F3...  26.3 us
    all_to_all x1, starting transfers between devices, on_device(): lax.all_to_all(outgoing, axes, split_axis=0, concat_axis=0, tiled=True)  11.5 us
    unnamed x21, local copies, waits for them, and re-layouts  6.73 us
    gather x1, local copies, waits for them, and re-layouts, on_device(): outgoing = features[send_rows[0]]  5.65 us
  transfers between devices with their start and end apart: 1, of which 0 were waited for; matrix products, arithmetic and copies ran while one was open for 1% of the time, Pallas kernels for 35%

profile of v2, /device:TPU:1, one launch (start us, length us, event | category | flops | bytes accessed | tf_op | source)
XLA Modules:
  0.0 148.4 jit_solution(557124481337642763)
XLA Ops:
  0.6 0.7 compare_select_fusion
  1.3 0.7 iota_compare_fusion
  2.1 0.1 copy.17
  2.2 0.1 reshape.100
  2.3 5.7 %gather_fusion = f32[1024,256]{1,0:T(8,128)S(1)} fusion(f32[4096,256]{1,0:T(8,128)} %feat_hbm.1, s32[1024]{0:T(1024)S(1)} %broadcast_clamp_fusion), kind=kCustom, calls=%fused_computation | custom fusion | bytes 2101248 | tf_op jit(solution)/shard_map/gather | solution.py:522
  7.9 1.2 bitcast_select_fusion
  9.1 11.5 %all-to-all-start = ((f32[128,8,256]{2,1,0:T(8,128)}), f32[128,8,256]{2,1,0:T(8,128)S(1)}, u32[]{:S(2)}, u32[]{:S(2)}) async-start(f32[128,8,256]{2,1,0:T(8,128)} %bitcast_select_fusion), calls=%async_computation | async-start | bytes 2097152 | tf_op jit(solution)/shard_map/all_to_all | solution.py:525
  21.9 0.9 constant_dynamic-slice_fusion
  22.8 0.1 copy.20
  22.9 0.8 copy.19
  23.7 0.0 copy-start.4
  23.7 0.0 copy-start.5
  23.7 0.0 copy-start.6
  23.8 51.2 %gather_hubs.1 = f32[2,4,4,4,256,128]{5,4,3,2,1,0:T(8,128)} custom-call(f32[256,128]{1,0:T(8,128)} %bitcast.24), custom_call_target="tpu_custom_call" | custom-call | tf_op jit(solution)/shard_map/gather_hubs/pallas_call | solution.py:176
  75.0 0.0 copy-done.7
  75.0 0.0 all-to-all-done
  75.0 0.0 copy-done.1
  75.1 40.3 %layer.1.grad_ref = f32[1032,128]{1,0:T(8,128)S(1)} custom-call(s32[128]{0:T(128)S(1)} %copy-done.6, s32[128]{0:T(128)S(1)} %compare_select_fusion.1.src_ref, s32[1]{0:T(128)S(6)} %copy.25.count_ref, f32[4096,256]{1,0:T(8,128)} %feat_hbm.1, f32[8,128,256]{2,1,0:T(8,128)S(1)} %bitcast.19, f32[128,256,128]{2,1,0:T(8,128)} %bitcast.23, ...), custom_call_target="tpu_custom_call" | custom-call | tf_op jit(solution)/shard_map/layer/pallas_call | solution.py:353
  115.4 0.8 copy-done
  116.2 26.3 %sum_grads.1 = (f32[256,256]{1,0:T(8,128)}, f32[256,256]{1,0:T(8,128)}, f32[1,256]{1,0:T(1,128)}, f32[1,256]{1,0:T(1,128)}) custom-call(f32[1032,128]{1,0:T(8,128)} %copy-done), custom_call_target="tpu_custom_call" | custom-call | tf_op jit(solution)/shard_map/sum_grads/pallas_call | solution.py:473
  142.6 1.7 %copy.27 = f32[256,256]{1,0:T(8,128)} copy(f32[256,256]{1,0:T(8,128)} %get-tuple-element.16) | data formatting | bytes 524288
  144.2 1.7 %copy.28 = f32[256,256]{1,0:T(8,128)} copy(f32[256,256]{1,0:T(8,128)} %get-tuple-element.17) | data formatting | bytes 524288
  145.9 1.2 copy.29
  147.1 1.2 copy.30
  (12 shorter events, 0.0 us)
Async XLA Ops:
  9.1 65.9 %all-to-all-start = ((f32[128,8,256]{2,1,0:T(8,128)}), f32[128,8,256]{2,1,0:T(8,128)S(1)}, u32[]{:S(2)}, u32[]{:S(2)}) async-start(f32[128,8,256]{2,1,0:T(8,128)} %bitcast_select_fusion), calls=%async_computation | async-start | bytes 2097152 | tf_op jit(solution)/shard_map/all_to_all | solution.py:525
  23.7 51.3 %copy-start.7 = (s32[128]{0:T(128)S(1)}, s32[128]{0:T(128)}, u32[]{:S(2)}) copy-start(s32[128]{0:T(128)} %param.20) | copy-start | bytes 1540
  23.7 51.3 %copy-start.1 = (f32[256,256]{1,0:T(8,128)S(1)}, f32[256,256]{1,0:T(8,128)}, u32[]{:S(2)}) copy-start(f32[256,256]{1,0:T(8,128)} %w_self_ref.1) | copy-start | bytes 786436
  23.7 51.3 %copy-start.2 = (f32[256,256]{1,0:T(8,128)S(1)}, f32[256,256]{1,0:T(8,128)}, u32[]{:S(2)}) copy-start(f32[256,256]{1,0:T(8,128)} %w_neigh_ref.1) | copy-start | bytes 786436
  23.7 51.3 %copy-start.3 = (s32[4096]{0:T(1024)S(1)}, s32[4096]{0:T(1024)}, u32[]{:S(2)}) copy-start(s32[4096]{0:T(1024)} %param.25) | copy-start | bytes 49156
  23.7 51.3 %copy-start.4 = (f32[256]{0:T(256)S(1)}, f32[256]{0:T(256)}, u32[]{:S(2)}) copy-start(f32[256]{0:T(256)} %param.16) | copy-start | bytes 3076
  23.7 51.3 %copy-start.5 = (f32[256]{0:T(256)S(1)}, f32[256]{0:T(256)}, u32[]{:S(2)}) copy-start(f32[256]{0:T(256)} %param.17) | copy-start | bytes 3076
  23.7 51.3 %copy-start.6 = (s32[128]{0:T(128)S(1)}, s32[128]{0:T(128)}, u32[]{:S(2)}) copy-start(s32[128]{0:T(128)} %dst_ref.1) | copy-start | bytes 1540
  115.4 0.8 copy-start

commit v3 on v2

v3 whole, which is shorter than its diff:
```python
import functools
import math

import jax
import jax.numpy as jnp
from jax import lax
from jax.experimental import pallas as pl
from jax.experimental.pallas import tpu as pltpu
from jax.sharding import PartitionSpec as P

MESH = pl.DeviceIdType.MESH
BF16 = jnp.bfloat16
F32 = jnp.float32

PART_START = (0, 88, 176)
PART_ROWS = (88, 88, 80)
PART_HALF = (48, 40, 40)
PART_AXES = ("xyz", "yzx", "zxy")
OFFSETS = (0, 3, 1, 2)


def my_place():
    vert = lax.axis_index("vert")
    row = lax.axis_index("row")
    core = lax.rem(vert, 2)
    x = lax.rem(lax.div(vert, 2), 4)
    y = lax.rem(lax.div(vert, 8), 2) * 2 + row
    z = lax.div(vert, 16)
    return {"x": x, "y": y, "z": z}, core


def device_at(place, core):
    x, y, z = place["x"], place["y"], place["z"]
    vert = ((z * 2 + lax.div(y, 2)) * 4 + x) * 2 + core
    return (vert, lax.rem(y, 2))


def shifted(place, axis, step):
    moved = dict(place)
    moved[axis] = lax.rem(place[axis] + step, 4)
    return moved


def split(value):
    high = value.astype(BF16)
    low = (value - high.astype(F32)).astype(BF16)
    return high, low


def dot(a, b, dims=(((1,), (0,)), ((), ()))):
    return lax.dot_general(a, b, dims, preferred_element_type=F32)


CHUNK = 256
TILE_CHUNK = 8
TILE_SLOTS = 4


def gather_kernel(
    hub_block_ref, rows_ref, count_ref, feat_hbm, weights_hbm, w_self_ref, bias_ref,
    table_ref, local_ref, split_ref, sums_ref,
    hub, self_k, ring, out_core, by_core, by_x, by_y, by_z,
    own_sem, feat_sem, ring_sem, recv1, recv2, recv3, send1, send2, send3, pair_send, pair_recv,
    border_send, border_recv, border_own,
):
    place, core = my_place()
    x, y, z = place["x"], place["y"], place["z"]
    near = {}
    for axis in "xyz":
        for step in (1, 2, 3):
            near[axis, step] = device_at(shifted(place, axis, step), core)
    sibling = device_at(place, 1 - core)

    loads = []
    for side in range(2):
        load = pltpu.make_async_copy(
            feat_hbm.at[:, :, pl.ds(128 * side, 128)],
            local_ref.at[pl.ds(0, 32), pl.ds(128 * side, 128), :],
            feat_sem.at[side],
        )
        load.start()
        loads.append(load)

    def load_tiles(i):
        spot = lax.rem(i, TILE_SLOTS)
        return pltpu.make_async_copy(
            weights_hbm.at[pl.ds(i * TILE_CHUNK, TILE_CHUNK)], ring.at[spot], ring_sem.at[spot]
        )

    for i in range(TILE_SLOTS):
        load_tiles(i).start()

    barrier = pltpu.get_barrier_semaphore()
    targets = list(near.values()) + [sibling]
    for target in targets:
        pl.semaphore_signal(barrier, inc=1, device_id=target, device_id_type=MESH)

    for load in loads:
        load.wait()
    hub[...] = local_ref[hub_block_ref[0]]
    own = pltpu.make_async_copy(hub, table_ref.at[core, z, y, x], own_sem)
    own.start()
    pl.semaphore_wait(barrier, len(targets))

    def slot(part, where, half=None):
        start, rows = PART_START[part], PART_ROWS[part]
        if half == 0:
            rows = PART_HALF[part]
        elif half == 1:
            start, rows = start + PART_HALF[part], rows - PART_HALF[part]
        at = []
        for axis in "zyx":
            offset = where.get(axis, 0)
            at.append(pl.ds(0, 4) if offset == "all" else lax.rem(place[axis] + offset, 4))
        return table_ref.at[(core, *at, pl.ds(start, rows), slice(None))]

    def remote(src, dst, send_sem, recv_sem, target):
        return pltpu.make_async_remote_copy(
            src_ref=src, dst_ref=dst, send_sem=send_sem, recv_sem=recv_sem,
            device_id=target, device_id_type=MESH,
        )

    def send_both(part, where, axis, send_sem, recv):
        dst = slot(part, where)
        src = dst if where else hub.at[pl.ds(PART_START[part], PART_ROWS[part])]
        remote(src, dst, send_sem, recv.at[0], near[axis, 1]).start()
        remote(src, dst, send_sem, recv.at[1], near[axis, 3]).start()

    def arrived(part, where, axis, sem, half=None):
        ref = slot(part, where, half)
        remote(ref, ref, sem, sem, near[axis, 1]).wait_recv()

    def pass_on(part, where, axis, send_sem, recv, half):
        ref = slot(part, where, half)
        remote(ref, ref, send_sem, recv.at[2 + half], near[axis, 1 if half == 0 else 3]).start()

    def to_sibling(part, where):
        ref = slot(part, where)
        remote(ref, ref, pair_send, pair_recv, sibling).start()

    parts = range(3)

    slot_row = lax.broadcasted_iota(jnp.int32, (8, 128), 0)

    def pick_rows(to_core, store):
        @pl.loop(0, 64)
        def _(i):
            y_low = lax.rem(i, 2)
            to_x = lax.rem(lax.div(i, 2), 4)
            y_high = lax.rem(lax.div(i, 8), 2)
            to_z = lax.div(i, 16)
            number = ((to_z * 2 + y_high) * 4 + to_x) * 4 + to_core * 2 + y_low
            alive = slot_row < count_ref[0, number]
            refs = [store(to_z, y_high, side, to_x, y_low) for side in range(2)]
            for k in range(8):
                row = rows_ref[0, number, k]
                block = lax.shift_right_logical(row, 7)
                inside = row & 127
                for side in range(2):
                    refs[side][pl.ds(k, 1), :] = local_ref[block, pl.ds(inside + 128 * side, 1), :]
            for side in range(2):
                refs[side][...] = jnp.where(alive, refs[side][...], 0.0)

    def border_go(stage, src, dst, target):
        remote(src, dst, border_send.at[stage], border_recv.at[stage], target).start()

    def border_wait(stage, ref):
        pltpu.make_async_copy(ref, ref, border_recv.at[stage]).wait()

    def border_core():
        border_go(0, out_core, by_core.at[:, :, :, :, core], sibling)

    def border_x():
        border_wait(0, out_core)
        keep = pltpu.make_async_copy(by_core.at[:, :, :, x], by_x.at[:, :, :, x], border_own.at[0])
        keep.start()
        for step in (1, 2, 3):
            border_go(1, by_core.at[:, :, :, lax.rem(x + step, 4)], by_x.at[:, :, :, x], near["x", step])
        keep.wait()

    def border_y():
        border_wait(1, by_x.at[pl.ds(0, 3)])
        yh, yl = lax.div(y, 2), lax.rem(y, 2)
        keep = pltpu.make_async_copy(
            by_x.at[:, yh, :, :, :, yl], by_y.at[:, yh, :, :, :, yl], border_own.at[1]
        )
        keep.start()
        for step in (1, 2, 3):
            to = lax.rem(y + step, 4)
            border_go(
                2, by_x.at[:, lax.div(to, 2), :, :, :, lax.rem(to, 2)],
                by_y.at[:, yh, :, :, :, yl], near["y", step],
            )
        keep.wait()

    def border_z():
        border_wait(2, by_y.at[pl.ds(0, 3)])
        keep = pltpu.make_async_copy(by_y.at[z], by_z.at[z], border_own.at[2])
        keep.start()
        for step in (1, 2, 3):
            border_go(3, by_y.at[lax.rem(z + step, 4)], by_z.at[z], near["z", step])
        keep.wait()

    def border_end():
        border_wait(3, by_z.at[pl.ds(0, 3)])
        for i in range(8):
            local_ref[32 + i] = by_z[i // 2, i % 2].reshape(256, 128)

    def pre_chunks(start, stop):
        @pl.loop(start, stop)
        def _(chunk):
            own = []
            for i in range(CHUNK // 128):
                block = local_ref[chunk * (CHUNK // 128) + i]
                own.append(jnp.concatenate([block[0:128], block[128:256]], axis=1))
            high, low = split(jnp.concatenate(own, axis=0))
            value = dot(jnp.concatenate([high, low, high], axis=1), self_k[...]) + bias_ref[...]
            for i in range(CHUNK // 128):
                for side in range(2):
                    local_ref[40 + chunk * (CHUNK // 128) + i, 128 * side:128 * side + 128, :] = value[
                        128 * i:128 * i + 128, 128 * side:128 * side + 128
                    ]

    lane = lax.broadcasted_iota(jnp.int32, (128, 128), 1)

    def tile_chunks(start, stop):
        @pl.loop(start, stop)
        def _(i):
            load_tiles(i).wait()
            spot = lax.rem(i, TILE_SLOTS)
            sums = sums_ref[...]
            for k in range(TILE_CHUNK):
                tile = i * TILE_CHUNK + k
                weight = ring[spot, k]
                high, low = split(weight)
                split_ref[tile, :, 0:128] = high
                split_ref[tile, :, 128:256] = low
                sums = jnp.where(lane == tile, jnp.sum(weight, axis=1, keepdims=True), sums)
            sums_ref[...] = sums

            @pl.when(i + TILE_SLOTS < 128 // TILE_CHUNK)
            def _():
                load_tiles(i + TILE_SLOTS).start()

    for p in parts:
        first, second, _ = PART_AXES[p]
        send_both(p, {}, first, send1.at[p], recv1.at[p])
        send_both(p, {}, second, send2.at[p], recv2.at[p, 0])

    sums_ref[...] = jnp.zeros_like(sums_ref)
    pick_rows(1 - core, lambda tz, yh, side, tx, yl: out_core.at[tz, yh, side, tx, yl])
    border_core()

    own.wait()
    for side, offset in ((0, 3), (1, 1)):
        unit = OFFSETS.index(offset)
        for p in parts:
            first, second, _ = PART_AXES[p]
            where = {first: offset}
            arrived(p, where, first, recv1.at[p, side])
            pass_on(p, where, first, send1.at[p], recv1.at[p], side)
            send_both(p, where, second, send2.at[p], recv2.at[p, unit])
    pick_rows(core, lambda tz, yh, side, tx, yl: by_core.at[tz, yh, side, tx, core, yl])
    border_x()
    for p in parts:
        first, second, third = PART_AXES[p]
        where = {first: 2}
        arrived(p, where, first, recv1.at[p, 2], 0)
        arrived(p, where, first, recv1.at[p, 3], 1)
        send_both(p, where, second, send2.at[p], recv2.at[p, 3])
        line = {first: "all"}
        send_both(p, line, third, send3.at[p], recv3.at[p, 0])
        to_sibling(p, line)
    self_high, self_low = split(w_self_ref[...])
    self_k[0:256, :] = self_high
    self_k[256:512, :] = self_high
    self_k[512:768, :] = self_low

    for unit in range(4):
        if unit == 2:
            border_y()
        for side, offset in ((0, 3), (1, 1)):
            for p in parts:
                first, second, _ = PART_AXES[p]
                where = {first: OFFSETS[unit], second: offset}
                arrived(p, where, second, recv2.at[p, unit, side])
                pass_on(p, where, second, send2.at[p], recv2.at[p, unit], side)
    for side, offset in ((0, 3), (1, 1)):
        for p in parts:
            first, second, third = PART_AXES[p]
            line = {first: "all", second: offset}
            send_both(p, line, third, send3.at[p], recv3.at[p, 1 + side])
            to_sibling(p, line)
    border_z()
    for p in parts:
        first, second, third = PART_AXES[p]
        for unit in range(4):
            where = {first: OFFSETS[unit], second: 2}
            arrived(p, where, second, recv2.at[p, unit, 2], 0)
            arrived(p, where, second, recv2.at[p, unit, 3], 1)
        line = {first: "all", second: 2}
        send_both(p, line, third, send3.at[p], recv3.at[p, 3])
        to_sibling(p, line)

    for unit in range(4):
        pre_chunks(4 * unit, 4 * unit + 4)
        for side, offset in ((0, 3), (1, 1)):
            for p in parts:
                first, second, third = PART_AXES[p]
                line = {first: "all", second: OFFSETS[unit], third: offset}
                arrived(p, line, third, recv3.at[p, unit, side])
                pass_on(p, line, third, send3.at[p], recv3.at[p, unit], side)
                to_sibling(p, line)
        if unit < 2:
            tile_chunks(8 * unit, 8 * unit + 8)
        if unit == 2:
            border_end()
    for unit in range(4):
        for p in parts:
            first, second, third = PART_AXES[p]
            line = {first: "all", second: OFFSETS[unit], third: 2}
            arrived(p, line, third, recv3.at[p, unit, 2], 0)
            arrived(p, line, third, recv3.at[p, unit, 3], 1)
            to_sibling(p, line)

    for p in parts:
        rows = pl.ds(PART_START[p], PART_ROWS[p])
        for sem, ref in (
            (send1.at[p], table_ref.at[core, 0, 0, pl.ds(0, 3), rows, :]),
            (send2.at[p], table_ref.at[core, 0, pl.ds(0, 3), pl.ds(0, 4), rows, :]),
            (send3.at[p], table_ref.at[core, pl.ds(0, 3), pl.ds(0, 4), pl.ds(0, 4), rows, :]),
        ):
            pltpu.make_async_copy(ref, ref, sem).wait()
    for stage, ref in enumerate((out_core, by_x.at[pl.ds(0, 3)], by_y.at[pl.ds(0, 3)], by_z.at[pl.ds(0, 3)])):
        pltpu.make_async_copy(ref, ref, border_send.at[stage]).wait()
    mine, theirs = table_ref.at[core], table_ref.at[1 - core]
    pltpu.make_async_copy(mine, mine, pair_send).wait()
    pltpu.make_async_copy(theirs, theirs, pair_recv).wait()


def gather(hub_block, send_rows, send_count, features, weights, w_self, bias):
    dma = pltpu.SemaphoreType.DMA
    smem = pl.BlockSpec(memory_space=pltpu.SMEM)
    vmem = pl.BlockSpec(memory_space=pltpu.VMEM)
    hbm = pl.BlockSpec(memory_space=pl.ANY)
    border = pltpu.VMEM((4, 2, 2, 4, 2, 2, 8, 128), F32)
    return pl.pallas_call(
        gather_kernel,
        out_shape=(
            jax.ShapeDtypeStruct((2, 4, 4, 4, 256, 128), F32),
            pltpu.VMEM((72, 256, 128), F32),
            pltpu.VMEM((128, 128, 256), BF16),
            pltpu.VMEM((128, 128), F32),
        ),
        in_specs=[smem] * 3 + [hbm] * 2 + [vmem] * 2,
        out_specs=(hbm,) + (vmem,) * 3,
        scratch_shapes=[
            pltpu.VMEM((256, 128), F32),
            pltpu.VMEM((768, 256), BF16),
            pltpu.VMEM((TILE_SLOTS, TILE_CHUNK, 128, 128), F32),
            pltpu.VMEM((4, 2, 2, 4, 2, 8, 128), F32),
            border, border, border, border,
            dma, dma((2,)), dma((TILE_SLOTS,)), dma((3, 4)), dma((3, 4, 4)), dma((3, 4, 4)),
            dma((3,)), dma((3,)), dma((3,)), dma, dma,
            dma((4,)), dma((4,)), dma((3,)),
        ],
        compiler_params=pltpu.CompilerParams(
            collective_id=0, has_side_effects=True, vmem_limit_bytes=34 * 2**20
        ),
        name="gather",
    )(hub_block, send_rows, send_count, features, weights, w_self, bias)


GROUP = 4


def layer_kernel(
    loss_scale, dst_ref, src_ref, count_ref,
    table_hbm, local_ref, split_ref, sums_ref, dst_row_ref, w_neigh_ref, head_ref, labels_ref,
    grad_ref,
    table_ref, neigh_k, total, grad_self, grad_neigh, grad_small, near_tiles, hub_tiles, table_sem,
):
    tiles = split_ref.shape[0]
    blocks = total.shape[0] - 1
    first_hub = blocks + 8
    count = count_ref[0]

    table_loads = [
        pltpu.make_async_copy(table_hbm.at[i // 4, i % 4], table_ref.at[i // 4, i % 4], table_sem.at[i])
        for i in range(8)
    ]
    for load in table_loads:
        load.start()
    total[...] = jnp.zeros_like(total)
    neigh_high, neigh_low = split(w_neigh_ref[...])
    neigh_k[0:256, :] = neigh_high
    neigh_k[256:512, :] = neigh_high
    neigh_k[512:768, :] = neigh_low

    def sort_tile(tile, ends):
        near_end, hub_end = ends
        near_tiles[near_end] = tile
        hub_tiles[hub_end] = tile
        near = jnp.where(src_ref[tile] < first_hub, 1, 0)
        return near_end + near, hub_end + (1 - near)

    near_count, hub_count = lax.fori_loop(0, count, sort_tile, (0, 0))

    def wide(block):
        return jnp.concatenate([block[0:128], block[128:256]], axis=1)

    def near_source(src):
        return wide(local_ref[src])

    def hub_source(src):
        number = src - first_hub
        return wide(table_ref[
            lax.shift_right_logical(number, 1) & 1,
            lax.shift_right_logical(number, 5),
            (lax.shift_right_logical(number, 4) & 1) * 2 + (number & 1),
            lax.shift_right_logical(number, 2) & 3,
        ])

    for listed, amount, source in ((near_tiles, near_count, near_source), (hub_tiles, hub_count, hub_source)):
        if listed is hub_tiles:
            for load in table_loads:
                load.wait()

        @pl.loop(0, lax.div(amount + (GROUP - 1), GROUP))
        def _(group):
            products, targets = [], []
            for k in range(GROUP):
                at = group * GROUP + k
                tile = listed[jnp.minimum(at, amount - 1)]
                targets.append(jnp.where(at < amount, dst_ref[tile], blocks))
                weight = split_ref[tile]
                high, low = split(source(src_ref[tile]))
                products.append(
                    dot(
                        jnp.concatenate([weight, weight[:, 0:128]], axis=1),
                        jnp.concatenate([high, high, low], axis=0),
                    )
                )
            for k in range(GROUP):
                total[targets[k]] += products[k]

    by_lanes = (((1,), (1,)), ((), ()))
    tile_lane = lax.broadcasted_iota(jnp.int32, (blocks, tiles), 1)
    block_row = lax.broadcasted_iota(jnp.int32, (blocks, tiles), 0)
    chosen = (dst_row_ref[...] == block_row) & (tile_lane < count)
    chosen = jnp.where(chosen, 1.0, 0.0).astype(BF16)
    sums_high, sums_low = split(sums_ref[...])
    sums_rest = (sums_ref[...] - sums_high.astype(F32) - sums_low.astype(F32)).astype(BF16)
    scales = 1.0 / (
        1.0 + (dot(sums_high, chosen, by_lanes) + dot(sums_low, chosen, by_lanes) + dot(sums_rest, chosen, by_lanes))
    )
    target_columns = (2.0 * labels_ref[...].astype(F32) - 1.0).T
    lane = lax.broadcasted_iota(jnp.int32, target_columns.shape, 1)

    grad_self[...] = jnp.zeros_like(grad_self)
    grad_neigh[...] = jnp.zeros_like(grad_neigh)
    grad_small[...] = jnp.zeros_like(grad_small)
    per_chunk = CHUNK // 128

    @pl.loop(0, blocks // per_chunk)
    def _(chunk):
        rows = pl.ds(pl.multiple_of(chunk * CHUNK, CHUNK), CHUNK)
        own, mean, target, pre = [], [], [], []
        for i in range(per_chunk):
            b = chunk * per_chunk + i
            block = wide(local_ref[b])
            scale = jnp.sum(jnp.where(lane == b, scales, 0.0), axis=1, keepdims=True)
            own.append(block)
            pre.append(wide(local_ref[first_hub + b]))
            mean.append((block + total[b]) * scale)
            target.append(jnp.sum(jnp.where(lane == b, target_columns, 0.0), axis=1, keepdims=True))
        own, mean, target, pre = (jnp.concatenate(v, axis=0) for v in (own, mean, target, pre))
        own_high, own_low = split(own)
        mean_high, mean_low = split(mean)
        pre = pre + dot(jnp.concatenate([mean_high, mean_low, mean_high], axis=1), neigh_k[...])
        gate = jax.nn.sigmoid(pre)
        hidden = pre * gate
        score = jnp.sum(hidden * head_ref[...], axis=1, keepdims=True)
        dscore = (score - target) * loss_scale
        dpre = dscore * head_ref[...] * (gate * (1.0 + pre * (1.0 - gate)))
        d_high, d_low = split(dpre)
        by_rows = (((0,), (0,)), ((), ()))
        right = jnp.concatenate([d_high, d_high, d_low], axis=0)
        grad_self[...] += dot(jnp.concatenate([own_high, own_low, own_high], axis=0), right, by_rows)
        grad_neigh[...] += dot(jnp.concatenate([mean_high, mean_low, mean_high], axis=0), right, by_rows)
        grad_small[0:1, :] += jnp.sum(dpre, axis=0, keepdims=True)
        grad_small[1:2, :] += jnp.sum(hidden * dscore, axis=0, keepdims=True)

    for i, ref in enumerate((grad_self, grad_neigh)):
        for side in range(2):
            grad_ref[pl.ds(512 * i + 256 * side, 256), :] = ref[:, 128 * side:128 * side + 128]
    grad_ref[1024:1032, :] = jnp.zeros((8, 128), F32)
    for i in range(4):
        side = 128 * (i % 2)
        grad_ref[1024 + i:1025 + i, :] = grad_small[i // 2:i // 2 + 1, side:side + 128]


def layer(loss_scale, dst, src, count, table, local, weights, sums, w_neigh, head, labels):
    smem = pl.BlockSpec(memory_space=pltpu.SMEM)
    vmem = pl.BlockSpec(memory_space=pltpu.VMEM)
    width = w_neigh.shape[0]
    blocks = labels.shape[0]
    return pl.pallas_call(
        functools.partial(layer_kernel, loss_scale),
        out_shape=pltpu.VMEM((1032, 128), F32),
        in_specs=[smem] * 3 + [pl.BlockSpec(memory_space=pl.ANY)] + [vmem] * 7,
        out_specs=vmem,
        scratch_shapes=[
            pltpu.VMEM(table.shape, F32),
            pltpu.VMEM((3 * width, width), BF16),
            pltpu.VMEM((blocks + 1, 128, width), F32),
            pltpu.VMEM((width, width), F32),
            pltpu.VMEM((width, width), F32),
            pltpu.VMEM((8, width), F32),
            pltpu.SMEM((dst.shape[0] + 1,), jnp.int32),
            pltpu.SMEM((dst.shape[0] + 1,), jnp.int32),
            pltpu.SemaphoreType.DMA((8,)),
        ],
        compiler_params=pltpu.CompilerParams(vmem_limit_bytes=30 * 2**20),
        name="layer",
    )(dst, src, count, table, local, weights, sums, dst.reshape(1, -1), w_neigh, head, labels)


def sum_kernel(
    grad_ref, whole,
    pair_in, plane_out, plane_in, plane_sum, z_out, z_in, send_sem, recv_sem,
):
    place, core = my_place()
    q = place["y"] * 4 + place["x"]
    z = place["z"]
    sibling = device_at(place, 1 - core)

    def plane_peer(step):
        other = lax.rem(q + step, 16)
        return other, device_at({"x": lax.rem(other, 4), "y": lax.div(other, 4), "z": z}, core)

    def z_peer(step):
        other = lax.rem(z + step, 4)
        return other, device_at(shifted(place, "z", step), core)

    barrier = pltpu.get_barrier_semaphore()
    targets = [sibling] + [plane_peer(s)[1] for s in range(1, 16)] + [z_peer(s)[1] for s in range(1, 4)]
    for target in targets:
        pl.semaphore_signal(barrier, inc=1, device_id=target, device_id_type=MESH)
    pl.semaphore_wait(barrier, len(targets))

    def send(stage, src, dst, target):
        pltpu.make_async_remote_copy(
            src_ref=src, dst_ref=dst, send_sem=send_sem.at[stage], recv_sem=recv_sem.at[stage],
            device_id=target, device_id_type=MESH,
        ).start()

    def received(stage, ref):
        pltpu.make_async_copy(ref, ref, recv_sem.at[stage]).wait()

    half, other_half = core * 512, (1 - core) * 512
    send(0, grad_ref.at[pl.ds(other_half, 512)], pair_in.at[pl.ds(0, 512)], sibling)
    send(0, grad_ref.at[pl.ds(1024, 8)], pair_in.at[pl.ds(512, 8)], sibling)
    received(0, pair_in)

    small = grad_ref[1024:1032, :] + pair_in[512:520, :]
    for step in range(1, 17):
        other, target = plane_peer(step)
        row = pl.multiple_of(other * 32, 32)
        buffer = plane_in if step == 16 else plane_out
        buffer[other, 0:32, :] = grad_ref[pl.ds(half + row, 32), :] + pair_in[pl.ds(row, 32), :]
        buffer[other, 32:40, :] = small
        if step < 16:
            send(1, plane_out.at[other], plane_in.at[q], target)
    received(1, plane_in.at[pl.ds(0, 15)])
    value = plane_in[0]
    for i in range(1, 16):
        value = value + plane_in[i]
    plane_sum[...] = value

    for step in range(1, 5):
        other, target = z_peer(step)
        buffer = z_in if step == 4 else z_out
        buffer[other, 0:8, :] = plane_sum[pl.ds(pl.multiple_of(other * 8, 8), 8), :]
        buffer[other, 8:16, :] = plane_sum[32:40, :]
        if step < 4:
            send(2, z_out.at[other], z_in.at[z], target)
    received(2, z_in.at[pl.ds(0, 3)])
    value = (z_in[0] + z_in[1]) + (z_in[2] + z_in[3])

    lot = half + q * 32
    mine = pl.ds(pl.multiple_of(lot + z * 8, 8), 8)
    whole[mine, :] = value[0:8]
    for step in range(1, 4):
        send(3, whole.at[mine], whole.at[mine], z_peer(step)[1])
    received(3, whole.at[pl.ds(0, 24)])
    mine = pl.ds(pl.multiple_of(lot, 32), 32)
    for step in range(1, 16):
        send(4, whole.at[mine], whole.at[mine], plane_peer(step)[1])
    received(4, whole.at[pl.ds(0, 480)])
    mine = pl.ds(pl.multiple_of(half, 512), 512)
    send(5, whole.at[mine], whole.at[mine], sibling)
    whole[1024:1032, :] = value[8:16]
    received(5, whole.at[pl.ds(0, 512)])

    sent = (
        pair_in, plane_in.at[pl.ds(0, 15)], z_in.at[pl.ds(0, 3)],
        whole.at[pl.ds(0, 24)], whole.at[pl.ds(0, 480)], whole.at[pl.ds(0, 512)],
    )
    for stage, ref in enumerate(sent):
        pltpu.make_async_copy(ref, ref, send_sem.at[stage]).wait()


def sum_grads(grads):
    vmem = pl.BlockSpec(memory_space=pltpu.VMEM)
    dma = pltpu.SemaphoreType.DMA
    return pl.pallas_call(
        sum_kernel,
        out_shape=pltpu.VMEM((1032, 128), F32),
        in_specs=[vmem],
        out_specs=vmem,
        scratch_shapes=[
            pltpu.VMEM((520, 128), F32),
            pltpu.VMEM((16, 40, 128), F32),
            pltpu.VMEM((16, 40, 128), F32),
            pltpu.VMEM((40, 128), F32),
            pltpu.VMEM((4, 16, 128), F32),
            pltpu.VMEM((4, 16, 128), F32),
            dma((6,)),
            dma((6,)),
        ],
        compiler_params=pltpu.CompilerParams(
            collective_id=1, has_side_effects=True, vmem_limit_bytes=8 * 2**20
        ),
        name="sum_grads",
    )(grads)


def unpack_kernel(whole, self_ref, neigh_ref, bias_ref, head_ref):
    for i, ref in enumerate((self_ref, neigh_ref)):
        for side in range(2):
            ref[:, 128 * side:128 * side + 128] = whole[pl.ds(512 * i + 256 * side, 256), :]
    for i in range(4):
        ref = (bias_ref, head_ref)[i // 2]
        ref[128 * (i % 2):128 * (i % 2) + 128] = whole[1024 + i, :]


def unpack(whole):
    vmem = pl.BlockSpec(memory_space=pltpu.VMEM)
    return pl.pallas_call(
        unpack_kernel,
        out_shape=(
            jax.ShapeDtypeStruct((256, 256), F32),
            jax.ShapeDtypeStruct((256, 256), F32),
            jax.ShapeDtypeStruct((256,), F32),
            jax.ShapeDtypeStruct((256,), F32),
        ),
        in_specs=[vmem],
        out_specs=(vmem,) * 4,
        compiler_params=pltpu.CompilerParams(vmem_limit_bytes=4 * 2**20),
        name="unpack",
    )(whole)


def on_device(
    features,
    w_self,
    w_neigh,
    bias,
    w_head,
    tile_weights,
    tile_dst,
    tile_src,
    tile_count,
    hub_block,
    send_rows,
    send_count,
    labels,
):
    width = features.shape[1]
    blocks = features.shape[0] // 128
    vertex_total = features.shape[0] * lax.axis_size(("vert", "row"))
    loss_scale = 1.0 / math.sqrt(vertex_total)
    table, local, weights, sums = gather(
        hub_block, send_rows, send_count, features.reshape(blocks, 128, width), tile_weights,
        w_self, bias.reshape(1, width),
    )
    grads = layer(
        loss_scale, tile_dst, tile_src, tile_count, table, local, weights, sums,
        w_neigh, w_head.reshape(1, width), labels.reshape(blocks, 128),
    )
    return unpack(sum_grads(grads))


def solution(mesh):
    in_specs = (
        P(("vert", "row"), None),
        P(),
        P(),
        P(),
        P(),
        P(("vert", "row"), None, None),
        P(("vert", "row")),
        P(("vert", "row")),
        P(("vert", "row")),
        P(("vert", "row")),
        P(("vert", "row"), None, None),
        P(("vert", "row"), None),
        P(("vert", "row")),
    )
    out_specs = (P(), P(), P(), P())
    return jax.shard_map(
        on_device, mesh=mesh, in_specs=in_specs, out_specs=out_specs, check_vma=False
    )
```

time: 149 us -> 132 us (0.89)
  starting transfers between devices: 11.5 us -> 0 us
  local copies, waits for them, and re-layouts: 14.2 us -> 3.09 us
  Pallas kernels: 118 us -> 126 us
  other arithmetic: 2.64 us -> 0 us
    all_to_all x1 -> x0, starting transfers between devices: 11.5 us -> none  [on_device(): lax.all_to_all(outgoing, axes, split_axis=0, concat_axis=0, tiled=True)]
    pallas_call x3 -> x4, Pallas kernels: 118 us -> 126 us  [the longest x1 71 us: gather(): pl.pallas_call(gather_kernel, out_shape=(jax.ShapeDtypeStruct((2, 4, 4, 4...]
    gather x1 -> x0, local copies, waits for them, and re-layouts: 5.65 us -> none  [on_device(): outgoing = features[send_rows[0]]]
    unnamed x21 -> x17, local copies, waits for them, and re-layouts: 6.73 us -> 3.09 us
    select_n x3 -> x0, other arithmetic: 1.89 us -> none  [the longest x1 1.19 us: on_device(): outgoing = jnp.where(alive[:, :, None], outgoing, jnp.zeros_like(outgoing))]
  transfers between devices with their start and end apart: 1 -> 0, of which waited for: 0 -> 0; matrix products, arithmetic and copies ran while one was open for 1% -> 0% of each run, Pallas kernels for 35% -> 0%
where the time goes in v3:
time: 132 us; the launch traced here: 131 us
  Pallas kernels  126 us (95%)
  local copies, waits for them, and re-layouts  3.09 us (2%)
  between operations  2.06 us (2%)
    pallas_call x1, Pallas kernels, gather(): pl.pallas_call(gather_kernel, out_shape=(jax.ShapeDtypeStruct((2, 4, 4, 4...  71 us
    pallas_call x1, Pallas kernels, sum_grads(): pl.pallas_call(sum_kernel, out_shape=pltpu.VMEM((1032, 128), F32), in_spe...  29.3 us
    pallas_call x1, Pallas kernels, layer(): pl.pallas_call(functools.partial(layer_kernel, loss_scale), out_shape=plt...  25.1 us
    unnamed x17, local copies, waits for them, and re-layouts  3.09 us

profile of v3, /device:TPU:1, one launch (start us, length us, event | category | flops | bytes accessed | tf_op | source)
XLA Modules:
  0.0 131.3 jit_solution(6986541004123274019)
XLA Ops:
  0.6 0.0 copy-start.3
  0.6 0.0 copy-start.2
  0.7 0.0 copy-start.7
  0.7 0.0 copy-start.4
  2.0 0.8 copy.17.rows_ref
  2.8 0.0 copy-start
  2.8 0.9 copy-done
  3.7 0.0 copy-start.5
  3.7 0.7 copy-done.5
  4.4 0.0 copy-start.6
  4.4 0.7 copy-done.6
  5.1 0.0 copy-start.1
  5.1 71.0 %gather.1 = (f32[2,4,4,4,256,128]{5,4,3,2,1,0:T(8,128)}, f32[72,256,128]{2,1,0:T(8,128)S(1)}, bf16[128,128,256]{2,1,0:T(8,128)(2,1)S(1)}, f32[128,128]{1,0:T(8,128)S(1)}) custom-call(s32[1]{0:T(128)S(6)} %copy.19.hub_block_ref, s32[1,128,8]{2,1,0:T(8,128)S(1)} %copy.17.rows_ref, s32[1,128]{1,0:T(1,128)S(1)} %copy-done.6, f32[32,128,256]{2,1,0:T(8,128)} %bitcast.9, ...), custom_call_target="tpu_custom_call" | custom-call | tf_op jit(solution)/shard_map/gather/pallas_call | solution.py:347
  76.0 0.0 copy-done.3
  76.1 0.0 copy-done.2
  76.1 0.0 copy-done.7
  76.1 0.0 copy-done.4
  76.1 0.0 copy-done.1
  76.1 25.1 %layer.1.grad_ref = f32[1032,128]{1,0:T(8,128)S(1)} custom-call(s32[128]{0:T(128)S(1)} %copy-done.3, s32[128]{0:T(128)S(1)} %copy-done.7, s32[1]{0:T(128)S(6)} %copy.18.count_ref, f32[2,4,4,4,256,128]{5,4,3,2,1,0:T(8,128)} %get-tuple-element.8.table_hbm, f32[72,256,128]{2,1,0:T(8,128)S(1)} %get-tuple-element.9.local_ref, ...), custom_call_target="tpu_custom_call" | custom-call | tf_op jit(solution)/shard_map/layer/pallas_call | solution.py:508
  101.2 29.3 %sum_grads.1.whole = f32[1032,128]{1,0:T(8,128)S(1)} custom-call(f32[1032,128]{1,0:T(8,128)S(1)} %layer.1.grad_ref), custom_call_target="tpu_custom_call" | custom-call | tf_op jit(solution)/shard_map/sum_grads/pallas_call | solution.py:617
  130.5 0.8 unpack.1
Async XLA Ops:
  0.6 75.4 %copy-start.3 = (s32[128]{0:T(128)S(1)}, s32[128]{0:T(128)}, u32[]{:S(2)}) copy-start(s32[128]{0:T(128)} %dst_ref.1) | copy-start | bytes 1540
  0.6 75.4 %copy-start.2 = (s32[4096]{0:T(1024)S(1)}, s32[4096]{0:T(1024)}, u32[]{:S(2)}) copy-start(s32[4096]{0:T(1024)} %param.25) | copy-start | bytes 49156
  0.7 75.4 %copy-start.7 = (s32[128]{0:T(128)S(1)}, s32[128]{0:T(128)}, u32[]{:S(2)}) copy-start(s32[128]{0:T(128)} %src_ref.1) | copy-start | bytes 1540
  0.7 75.4 %copy-start.4 = (f32[256]{0:T(256)S(1)}, f32[256]{0:T(256)}, u32[]{:S(2)}) copy-start(f32[256]{0:T(256)} %param.17) | copy-start | bytes 3076
  2.8 0.9 copy-start
  3.7 0.7 copy-start.5
  4.4 0.7 copy-start.6
  5.1 71.0 %copy-start.1 = (f32[256,256]{1,0:T(8,128)S(1)}, f32[256,256]{1,0:T(8,128)}, u32[]{:S(2)}) copy-start(f32[256,256]{1,0:T(8,128)} %w_neigh_ref.1) | copy-start | bytes 786436

commit v4 on v3

--- a/solution.py
+++ b/solution.py
@@ -59,17 +59,22 @@
 def gather_kernel(
     hub_block_ref, rows_ref, count_ref, feat_hbm, weights_hbm, w_self_ref, bias_ref,
     table_ref, local_ref, split_ref, sums_ref,
-    hub, self_k, ring, out_core, by_core, by_x, by_y, by_z,
+    hub, self_k, ring, outbox, inbox,
     own_sem, feat_sem, ring_sem, recv1, recv2, recv3, send1, send2, send3, pair_send, pair_recv,
-    border_send, border_recv, border_own,
+    border_send, border_recv,
 ):
     place, core = my_place()
     x, y, z = place["x"], place["y"], place["z"]
     near = {}
     for axis in "xyz":
-        for step in (1, 2, 3):
+        for step in (1, 3):
             near[axis, step] = device_at(shifted(place, axis, step), core)
     sibling = device_at(place, 1 - core)
+    me = lax.axis_index("vert") * 2 + lax.axis_index("row")
+
+    def other(step):
+        number = lax.rem(me + step, 128)
+        return number, (lax.div(number, 2), lax.rem(number, 2))
 
     loads = []
     for side in range(2):
@@ -91,16 +96,18 @@
         load_tiles(i).start()
 
     barrier = pltpu.get_barrier_semaphore()
-    targets = list(near.values()) + [sibling]
-    for target in targets:
-        pl.semaphore_signal(barrier, inc=1, device_id=target, device_id_type=MESH)
+
+    @pl.loop(1, 128)
+    def _(step):
+        pl.semaphore_signal(barrier, inc=1, device_id=other(step)[1], device_id_type=MESH)
+
 
     for load in loads:
         load.wait()
     hub[...] = local_ref[hub_block_ref[0]]
     own = pltpu.make_async_copy(hub, table_ref.at[core, z, y, x], own_sem)
     own.start()
-    pl.semaphore_wait(barrier, len(targets))
+    pl.semaphore_wait(barrier, 127)
 
     def slot(part, where, half=None):
         start, rows = PART_START[part], PART_ROWS[part]
@@ -142,69 +149,33 @@
 
     slot_row = lax.broadcasted_iota(jnp.int32, (8, 128), 0)
 
-    def pick_rows(to_core, store):
-        @pl.loop(0, 64)
-        def _(i):
-            y_low = lax.rem(i, 2)
-            to_x = lax.rem(lax.div(i, 2), 4)
-            y_high = lax.rem(lax.div(i, 8), 2)
-            to_z = lax.div(i, 16)
-            number = ((to_z * 2 + y_high) * 4 + to_x) * 4 + to_core * 2 + y_low
+    def border_go(first, stop):
+        @pl.loop(first, stop)
+        def _(step):
+            number, target = other(step)
             alive = slot_row < count_ref[0, number]
-            refs = [store(to_z, y_high, side, to_x, y_low) for side in range(2)]
             for k in range(8):
                 row = rows_ref[0, number, k]
                 block = lax.shift_right_logical(row, 7)
                 inside = row & 127
                 for side in range(2):
-                    refs[side][pl.ds(k, 1), :] = local_ref[block, pl.ds(inside + 128 * side, 1), :]
+                    outbox[number, side, pl.ds(k, 1), :] = local_ref[block, pl.ds(inside + 128 * side, 1), :]
             for side in range(2):
-                refs[side][...] = jnp.where(alive, refs[side][...], 0.0)
-
-    def border_go(stage, src, dst, target):
-        remote(src, dst, border_send.at[stage], border_recv.at[stage], target).start()
-
-    def border_wait(stage, ref):
-        pltpu.make_async_copy(ref, ref, border_recv.at[stage]).wait()
-
-    def border_core():
-        border_go(0, out_core, by_core.at[:, :, :, :, core], sibling)
-
-    def border_x():
-        border_wait(0, out_core)
-        keep = pltpu.make_async_copy(by_core.at[:, :, :, x], by_x.at[:, :, :, x], border_own.at[0])
-        keep.start()
-        for step in (1, 2, 3):
-            border_go(1, by_core.at[:, :, :, lax.rem(x + step, 4)], by_x.at[:, :, :, x], near["x", step])
-        keep.wait()
-
-    def border_y():
-        border_wait(1, by_x.at[pl.ds(0, 3)])
-        yh, yl = lax.div(y, 2), lax.rem(y, 2)
-        keep = pltpu.make_async_copy(
-            by_x.at[:, yh, :, :, :, yl], by_y.at[:, yh, :, :, :, yl], border_own.at[1]
-        )
-        keep.start()
-        for step in (1, 2, 3):
-            to = lax.rem(y + step, 4)
-            border_go(
-                2, by_x.at[:, lax.div(to, 2), :, :, :, lax.rem(to, 2)],
-                by_y.at[:, yh, :, :, :, yl], near["y", step],
-            )
-        keep.wait()
-
-    def border_z():
-        border_wait(2, by_y.at[pl.ds(0, 3)])
-        keep = pltpu.make_async_copy(by_y.at[z], by_z.at[z], border_own.at[2])
-        keep.start()
-        for step in (1, 2, 3):
-            border_go(3, by_y.at[lax.rem(z + step, 4)], by_z.at[z], near["z", step])
-        keep.wait()
+                outbox[number, side] = jnp.where(alive, outbox[number, side], 0.0)
+            if first == 128:
+                inbox[number] = outbox[number]
+            else:
+                remote(outbox.at[number], inbox.at[me], border_send, border_recv, target).start()
 
     def border_end():
-        border_wait(3, by_z.at[pl.ds(0, 3)])
-        for i in range(8):
-            local_ref[32 + i] = by_z[i // 2, i % 2].reshape(256, 128)
+        arrived_all = inbox.at[pl.ds(0, 127)]
+        pltpu.make_async_copy(arrived_all, arrived_all, border_recv).wait()
+
+        @pl.loop(0, 8)
+        def _(i):
+            for k in range(16):
+                for side in range(2):
+                    local_ref[32 + i, 128 * side + 8 * k:128 * side + 8 * k + 8, :] = inbox[16 * i + k, side]
 
     def pre_chunks(start, stop):
         @pl.loop(start, stop)
@@ -248,9 +219,7 @@
         send_both(p, {}, second, send2.at[p], recv2.at[p, 0])
 
     sums_ref[...] = jnp.zeros_like(sums_ref)
-    pick_rows(1 - core, lambda tz, yh, side, tx, yl: out_core.at[tz, yh, side, tx, yl])
-    border_core()
-
+    border_go(1, 65)
     own.wait()
     for side, offset in ((0, 3), (1, 1)):
         unit = OFFSETS.index(offset)
@@ -260,8 +229,8 @@
             arrived(p, where, first, recv1.at[p, side])
             pass_on(p, where, first, send1.at[p], recv1.at[p], side)
             send_both(p, where, second, send2.at[p], recv2.at[p, unit])
-    pick_rows(core, lambda tz, yh, side, tx, yl: by_core.at[tz, yh, side, tx, core, yl])
-    border_x()
+    border_go(65, 128)
+    border_go(128, 129)
     for p in parts:
         first, second, third = PART_AXES[p]
         where = {first: 2}
@@ -277,8 +246,6 @@
     self_k[512:768, :] = self_low
 
     for unit in range(4):
-        if unit == 2:
-            border_y()
         for side, offset in ((0, 3), (1, 1)):
             for p in parts:
                 first, second, _ = PART_AXES[p]
@@ -291,7 +258,6 @@
             line = {first: "all", second: offset}
             send_both(p, line, third, send3.at[p], recv3.at[p, 1 + side])
             to_sibling(p, line)
-    border_z()
     for p in parts:
         first, second, third = PART_AXES[p]
         for unit in range(4):
@@ -331,8 +297,8 @@
             (send3.at[p], table_ref.at[core, pl.ds(0, 3), pl.ds(0, 4), pl.ds(0, 4), rows, :]),
         ):
             pltpu.make_async_copy(ref, ref, sem).wait()
-    for stage, ref in enumerate((out_core, by_x.at[pl.ds(0, 3)], by_y.at[pl.ds(0, 3)], by_z.at[pl.ds(0, 3)])):
-        pltpu.make_async_copy(ref, ref, border_send.at[stage]).wait()
+    sent = outbox.at[pl.ds(0, 127)]
+    pltpu.make_async_copy(sent, sent, border_send).wait()
     mine, theirs = table_ref.at[core], table_ref.at[1 - core]
     pltpu.make_async_copy(mine, mine, pair_send).wait()
     pltpu.make_async_copy(theirs, theirs, pair_recv).wait()
@@ -343,7 +309,7 @@
     smem = pl.BlockSpec(memory_space=pltpu.SMEM)
     vmem = pl.BlockSpec(memory_space=pltpu.VMEM)
     hbm = pl.BlockSpec(memory_space=pl.ANY)
-    border = pltpu.VMEM((4, 2, 2, 4, 2, 2, 8, 128), F32)
+    border = pltpu.VMEM((128, 2, 8, 128), F32)
     return pl.pallas_call(
         gather_kernel,
         out_shape=(
@@ -358,11 +324,10 @@
             pltpu.VMEM((256, 128), F32),
             pltpu.VMEM((768, 256), BF16),
             pltpu.VMEM((TILE_SLOTS, TILE_CHUNK, 128, 128), F32),
-            pltpu.VMEM((4, 2, 2, 4, 2, 8, 128), F32),
-            border, border, border, border,
+            border, border,
             dma, dma((2,)), dma((TILE_SLOTS,)), dma((3, 4)), dma((3, 4, 4)), dma((3, 4, 4)),
             dma((3,)), dma((3,)), dma((3,)), dma, dma,
-            dma((4,)), dma((4,)), dma((3,)),
+            dma, dma,
         ],
         compiler_params=pltpu.CompilerParams(
             collective_id=0, has_side_effects=True, vmem_limit_bytes=34 * 2**20

time: 132 us -> 126 us (0.955)
  Pallas kernels: 126 us -> 120 us
    pallas_call x1, Pallas kernels: 71 us -> 62.4 us  [gather(): pl.pallas_call(gather_kernel, out_shape=(jax.ShapeDtypeStruct((2, 4, 4, 4...]
    pallas_call x1, Pallas kernels: 29.3 us -> 31.8 us  [sum_grads(): pl.pallas_call(sum_kernel, out_shape=pltpu.VMEM((1032, 128), F32), in_spe...]
where the time goes in v4:
time: 126 us
  Pallas kernels  120 us (95%)
  local copies, waits for them, and re-layouts  3.09 us (2%)
  between operations  2.06 us (2%)
    pallas_call x1, Pallas kernels, gather(): pl.pallas_call(gather_kernel, out_shape=(jax.ShapeDtypeStruct((2, 4, 4, 4...  62.4 us
    pallas_call x1, Pallas kernels, sum_grads(): pl.pallas_call(sum_kernel, out_shape=pltpu.VMEM((1032, 128), F32), in_spe...  31.8 us
    pallas_call x1, Pallas kernels, layer(): pl.pallas_call(functools.partial(layer_kernel, loss_scale), out_shape=plt...  25.4 us
    unnamed x17, local copies, waits for them, and re-layouts  3.09 us

profile of v4, /device:TPU:1, one launch (start us, length us, event | category | flops | bytes accessed | tf_op | source)
XLA Modules:
  0.0 125.6 jit_solution(4803933304420869731)
XLA Ops:
  0.6 0.0 copy-start.3
  0.6 0.0 copy-start.2
  0.7 0.0 copy-start.7
  0.7 0.0 copy-start.4
  2.0 0.8 copy.17.rows_ref
  2.8 0.0 copy-start
  2.8 0.9 copy-done
  3.7 0.0 copy-start.5
  3.7 0.7 copy-done.5
  4.4 0.0 copy-start.6
  4.4 0.7 copy-done.6
  5.1 0.0 copy-start.1
  5.1 62.4 %gather.1 = (f32[2,4,4,4,256,128]{5,4,3,2,1,0:T(8,128)}, f32[72,256,128]{2,1,0:T(8,128)S(1)}, bf16[128,128,256]{2,1,0:T(8,128)(2,1)S(1)}, f32[128,128]{1,0:T(8,128)S(1)}) custom-call(s32[1]{0:T(128)S(6)} %copy.19.hub_block_ref, s32[1,128,8]{2,1,0:T(8,128)S(1)} %copy.17.rows_ref, s32[1,128]{1,0:T(1,128)S(1)} %copy-done.6, f32[32,128,256]{2,1,0:T(8,128)} %bitcast.9, ...), custom_call_target="tpu_custom_call" | custom-call | tf_op jit(solution)/shard_map/gather/pallas_call | solution.py:313
  67.5 0.0 copy-done.3
  67.5 0.0 copy-done.2
  67.5 0.0 copy-done.7
  67.5 0.0 copy-done.4
  67.5 0.0 copy-done.1
  67.5 25.4 %layer.1.grad_ref = f32[1032,128]{1,0:T(8,128)S(1)} custom-call(s32[128]{0:T(128)S(1)} %copy-done.3, s32[128]{0:T(128)S(1)} %copy-done.7, s32[1]{0:T(128)S(6)} %copy.18.count_ref, f32[2,4,4,4,256,128]{5,4,3,2,1,0:T(8,128)} %get-tuple-element.8.table_hbm, f32[72,256,128]{2,1,0:T(8,128)S(1)} %get-tuple-element.9.local_ref, ...), custom_call_target="tpu_custom_call" | custom-call | tf_op jit(solution)/shard_map/layer/pallas_call | solution.py:473
  93.0 31.8 %sum_grads.1.whole = f32[1032,128]{1,0:T(8,128)S(1)} custom-call(f32[1032,128]{1,0:T(8,128)S(1)} %layer.1.grad_ref), custom_call_target="tpu_custom_call" | custom-call | tf_op jit(solution)/shard_map/sum_grads/pallas_call | solution.py:582
  124.8 0.8 unpack.1
Async XLA Ops:
  0.6 66.9 %copy-start.3 = (s32[128]{0:T(128)S(1)}, s32[128]{0:T(128)}, u32[]{:S(2)}) copy-start(s32[128]{0:T(128)} %dst_ref.1) | copy-start | bytes 1540
  0.6 66.9 %copy-start.2 = (s32[4096]{0:T(1024)S(1)}, s32[4096]{0:T(1024)}, u32[]{:S(2)}) copy-start(s32[4096]{0:T(1024)} %param.25) | copy-start | bytes 49156
  0.7 66.9 %copy-start.7 = (s32[128]{0:T(128)S(1)}, s32[128]{0:T(128)}, u32[]{:S(2)}) copy-start(s32[128]{0:T(128)} %src_ref.1) | copy-start | bytes 1540
  0.7 66.9 %copy-start.4 = (f32[256]{0:T(256)S(1)}, f32[256]{0:T(256)}, u32[]{:S(2)}) copy-start(f32[256]{0:T(256)} %param.17) | copy-start | bytes 3076
  2.8 0.9 copy-start
  3.7 0.7 copy-start.5
  4.4 0.7 copy-start.6
  5.1 62.5 %copy-start.1 = (f32[256,256]{1,0:T(8,128)S(1)}, f32[256,256]{1,0:T(8,128)}, u32[]{:S(2)}) copy-start(f32[256,256]{1,0:T(8,128)} %w_neigh_ref.1) | copy-start | bytes 786436

commit v5 on v4

--- a/solution.py
+++ b/solution.py
@@ -51,6 +51,7 @@
     return lax.dot_general(a, b, dims, preferred_element_type=F32)
 
 
+GATHER_VMEM, TILES_VMEM, LAYER_VMEM = 34, 30, 30
 CHUNK = 256
 TILE_CHUNK = 8
 TILE_SLOTS = 4
@@ -330,7 +331,7 @@
             dma, dma,
         ],
         compiler_params=pltpu.CompilerParams(
-            collective_id=0, has_side_effects=True, vmem_limit_bytes=34 * 2**20
+            collective_id=0, has_side_effects=True, vmem_limit_bytes=GATHER_VMEM * 2**20
         ),
         name="gather",
     )(hub_block, send_rows, send_count, features, weights, w_self, bias)
@@ -339,11 +340,11 @@
 GROUP = 4
 
 
-def layer_kernel(
-    loss_scale, dst_ref, src_ref, count_ref,
-    table_hbm, local_ref, split_ref, sums_ref, dst_row_ref, w_neigh_ref, head_ref, labels_ref,
-    grad_ref,
-    table_ref, neigh_k, total, grad_self, grad_neigh, grad_small, near_tiles, hub_tiles, table_sem,
+def tiles_kernel(
+    dst_ref, src_ref, count_ref,
+    table_hbm, local_ref, split_ref, sums_ref, dst_row_ref,
+    total, scales_ref,
+    table_ref, near_tiles, low_tiles, high_tiles, table_sem,
 ):
     tiles = split_ref.shape[0]
     blocks = total.shape[0] - 1
@@ -357,19 +358,17 @@
     for load in table_loads:
         load.start()
     total[...] = jnp.zeros_like(total)
-    neigh_high, neigh_low = split(w_neigh_ref[...])
-    neigh_k[0:256, :] = neigh_high
-    neigh_k[256:512, :] = neigh_high
-    neigh_k[512:768, :] = neigh_low
 
     def sort_tile(tile, ends):
-        near_end, hub_end = ends
-        near_tiles[near_end] = tile
-        hub_tiles[hub_end] = tile
-        near = jnp.where(src_ref[tile] < first_hub, 1, 0)
-        return near_end + near, hub_end + (1 - near)
-
-    near_count, hub_count = lax.fori_loop(0, count, sort_tile, (0, 0))
+        src = src_ref[tile]
+        near = jnp.where(src < first_hub, 1, 0)
+        high = (1 - near) * (lax.shift_right_logical(src - first_hub, 1) & 1)
+        kinds = (near, 1 - near - high, high)
+        for listed, end in zip((near_tiles, low_tiles, high_tiles), ends):
+            listed[end] = tile
+        return tuple(end + kind for end, kind in zip(ends, kinds))
+
+    amounts = lax.fori_loop(0, count, sort_tile, (0, 0, 0))
 
     def wide(block):
         return jnp.concatenate([block[0:128], block[128:256]], axis=1)
@@ -386,10 +385,21 @@
             lax.shift_right_logical(number, 2) & 3,
         ])
 
-    for listed, amount, source in ((near_tiles, near_count, near_source), (hub_tiles, hub_count, hub_source)):
-        if listed is hub_tiles:
-            for load in table_loads:
-                load.wait()
+    by_lanes = (((1,), (1,)), ((), ()))
+    tile_lane = lax.broadcasted_iota(jnp.int32, (blocks, tiles), 1)
+    block_row = lax.broadcasted_iota(jnp.int32, (blocks, tiles), 0)
+    chosen = (dst_row_ref[...] == block_row) & (tile_lane < count)
+    chosen = jnp.where(chosen, 1.0, 0.0).astype(BF16)
+    sums_high, sums_low = split(sums_ref[...])
+    sums_rest = (sums_ref[...] - sums_high.astype(F32) - sums_low.astype(F32)).astype(BF16)
+    scales_ref[...] = 1.0 / (
+        1.0 + (dot(sums_high, chosen, by_lanes) + dot(sums_low, chosen, by_lanes) + dot(sums_rest, chosen, by_lanes))
+    )
+
+    work = ((near_tiles, near_source, ()), (low_tiles, hub_source, table_loads[:4]), (high_tiles, hub_source, table_loads[4:]))
+    for (listed, source, loads), amount in zip(work, amounts):
+        for load in loads:
+            load.wait()
 
         @pl.loop(0, lax.div(amount + (GROUP - 1), GROUP))
         def _(group):
@@ -409,34 +419,73 @@
             for k in range(GROUP):
                 total[targets[k]] += products[k]
 
-    by_lanes = (((1,), (1,)), ((), ()))
-    tile_lane = lax.broadcasted_iota(jnp.int32, (blocks, tiles), 1)
-    block_row = lax.broadcasted_iota(jnp.int32, (blocks, tiles), 0)
-    chosen = (dst_row_ref[...] == block_row) & (tile_lane < count)
-    chosen = jnp.where(chosen, 1.0, 0.0).astype(BF16)
-    sums_high, sums_low = split(sums_ref[...])
-    sums_rest = (sums_ref[...] - sums_high.astype(F32) - sums_low.astype(F32)).astype(BF16)
-    scales = 1.0 / (
-        1.0 + (dot(sums_high, chosen, by_lanes) + dot(sums_low, chosen, by_lanes) + dot(sums_rest, chosen, by_lanes))
-    )
+
+def add_tiles(dst, src, count, table, local, weights, sums, blocks):
+    smem = pl.BlockSpec(memory_space=pltpu.SMEM)
+    vmem = pl.BlockSpec(memory_space=pltpu.VMEM)
+    listed = pltpu.SMEM((dst.shape[0] + 1,), jnp.int32)
+    return pl.pallas_call(
+        tiles_kernel,
+        out_shape=(pltpu.VMEM((blocks + 1, 128, 256), F32), pltpu.VMEM((128, blocks), F32)),
+        in_specs=[smem] * 3 + [pl.BlockSpec(memory_space=pl.ANY)] + [vmem] * 4,
+        out_specs=(vmem, vmem),
+        scratch_shapes=[
+            pltpu.VMEM(table.shape, F32), listed, listed, listed, pltpu.SemaphoreType.DMA((8,)),
+        ],
+        compiler_params=pltpu.CompilerParams(vmem_limit_bytes=TILES_VMEM * 2**20),
+        name="add_tiles",
+    )(dst, src, count, table, local, weights, sums, dst.reshape(1, -1))
+
+
+LAYER_CHUNK = 512
+
+
+def layer_kernel(
+    loss_scale, total, scales_ref, local_ref, w_neigh_ref, head_ref, labels_ref,
+    whole,
+    neigh_k, grad_self, grad_neigh, grad_small, grads, pair_in, lots_in, small_in,
+    send_sem, recv_sem,
+):
+    place, core = my_place()
+    number = (place["z"] * 4 + place["y"]) * 4 + place["x"]
+    sibling = device_at(place, 1 - core)
+
+    def peer(step):
+        other = lax.rem(number + step, 64)
+        at = {"x": lax.rem(other, 4), "y": lax.rem(lax.div(other, 4), 4), "z": lax.div(other, 16)}
+        return other, device_at(at, core)
+
+    barrier = pltpu.get_barrier_semaphore()
+    pl.semaphore_signal(barrier, inc=1, device_id=sibling, device_id_type=MESH)
+
+    @pl.loop(1, 64)
+    def _(step):
+        pl.semaphore_signal(barrier, inc=1, device_id=peer(step)[1], device_id_type=MESH)
+
+    blocks = labels_ref.shape[0]
+    neigh_high, neigh_low = split(w_neigh_ref[...])
+    neigh_k[0:256, :] = neigh_high
+    neigh_k[256:512, :] = neigh_high
+    neigh_k[512:768, :] = neigh_low
     target_columns = (2.0 * labels_ref[...].astype(F32) - 1.0).T
     lane = lax.broadcasted_iota(jnp.int32, target_columns.shape, 1)
-
     grad_self[...] = jnp.zeros_like(grad_self)
     grad_neigh[...] = jnp.zeros_like(grad_neigh)
     grad_small[...] = jnp.zeros_like(grad_small)
-    per_chunk = CHUNK // 128
+    per_chunk = LAYER_CHUNK // 128
+
+    def wide(block):
+        return jnp.concatenate([block[0:128], block[128:256]], axis=1)
 
     @pl.loop(0, blocks // per_chunk)
     def _(chunk):
-        rows = pl.ds(pl.multiple_of(chunk * CHUNK, CHUNK), CHUNK)
         own, mean, target, pre = [], [], [], []
         for i in range(per_chunk):
             b = chunk * per_chunk + i
             block = wide(local_ref[b])
-            scale = jnp.sum(jnp.where(lane == b, scales, 0.0), axis=1, keepdims=True)
+            scale = jnp.sum(jnp.where(lane == b, scales_ref[...], 0.0), axis=1, keepdims=True)
             own.append(block)
-            pre.append(wide(local_ref[first_hub + b]))
+            pre.append(wide(local_ref[blocks + 8 + b]))
             mean.append((block + total[b]) * scale)
             target.append(jnp.sum(jnp.where(lane == b, target_columns, 0.0), axis=1, keepdims=True))
         own, mean, target, pre = (jnp.concatenate(v, axis=0) for v in (own, mean, target, pre))
@@ -458,61 +507,13 @@
 
     for i, ref in enumerate((grad_self, grad_neigh)):
         for side in range(2):
-            grad_ref[pl.ds(512 * i + 256 * side, 256), :] = ref[:, 128 * side:128 * side + 128]
-    grad_ref[1024:1032, :] = jnp.zeros((8, 128), F32)
+            grads[pl.ds(512 * i + 256 * side, 256), :] = ref[:, 128 * side:128 * side + 128]
+    grads[1024:1032, :] = jnp.zeros((8, 128), F32)
     for i in range(4):
         side = 128 * (i % 2)
-        grad_ref[1024 + i:1025 + i, :] = grad_small[i // 2:i // 2 + 1, side:side + 128]
-
-
-def layer(loss_scale, dst, src, count, table, local, weights, sums, w_neigh, head, labels):
-    smem = pl.BlockSpec(memory_space=pltpu.SMEM)
-    vmem = pl.BlockSpec(memory_space=pltpu.VMEM)
-    width = w_neigh.shape[0]
-    blocks = labels.shape[0]
-    return pl.pallas_call(
-        functools.partial(layer_kernel, loss_scale),
-        out_shape=pltpu.VMEM((1032, 128), F32),
-        in_specs=[smem] * 3 + [pl.BlockSpec(memory_space=pl.ANY)] + [vmem] * 7,
-        out_specs=vmem,
-        scratch_shapes=[
-            pltpu.VMEM(table.shape, F32),
-            pltpu.VMEM((3 * width, width), BF16),
-            pltpu.VMEM((blocks + 1, 128, width), F32),
-            pltpu.VMEM((width, width), F32),
-            pltpu.VMEM((width, width), F32),
-            pltpu.VMEM((8, width), F32),
-            pltpu.SMEM((dst.shape[0] + 1,), jnp.int32),
-            pltpu.SMEM((dst.shape[0] + 1,), jnp.int32),
-            pltpu.SemaphoreType.DMA((8,)),
-        ],
-        compiler_params=pltpu.CompilerParams(vmem_limit_bytes=30 * 2**20),
-        name="layer",
-    )(dst, src, count, table, local, weights, sums, dst.reshape(1, -1), w_neigh, head, labels)
-
-
-def sum_kernel(
-    grad_ref, whole,
-    pair_in, plane_out, plane_in, plane_sum, z_out, z_in, send_sem, recv_sem,
-):
-    place, core = my_place()
-    q = place["y"] * 4 + place["x"]
-    z = place["z"]
-    sibling = device_at(place, 1 - core)
-
-    def plane_peer(step):
-        other = lax.rem(q + step, 16)
-        return other, device_at({"x": lax.rem(other, 4), "y": lax.div(other, 4), "z": z}, core)
-
-    def z_peer(step):
-        other = lax.rem(z + step, 4)
-        return other, device_at(shifted(place, "z", step), core)
-
-    barrier = pltpu.get_barrier_semaphore()
-    targets = [sibling] + [plane_peer(s)[1] for s in range(1, 16)] + [z_peer(s)[1] for s in range(1, 4)]
-    for target in targets:
-        pl.semaphore_signal(barrier, inc=1, device_id=target, device_id_type=MESH)
-    pl.semaphore_wait(barrier, len(targets))
+        grads[1024 + i:1025 + i, :] = grad_small[i // 2:i // 2 + 1, side:side + 128]
+
+    pl.semaphore_wait(barrier, 64)
 
     def send(stage, src, dst, target):
         pltpu.make_async_remote_copy(
@@ -523,82 +524,112 @@
     def received(stage, ref):
         pltpu.make_async_copy(ref, ref, recv_sem.at[stage]).wait()
 
+    def sent(stage, ref):
+        pltpu.make_async_copy(ref, ref, send_sem.at[stage]).wait()
+
     half, other_half = core * 512, (1 - core) * 512
-    send(0, grad_ref.at[pl.ds(other_half, 512)], pair_in.at[pl.ds(0, 512)], sibling)
-    send(0, grad_ref.at[pl.ds(1024, 8)], pair_in.at[pl.ds(512, 8)], sibling)
+    small = pl.ds(1024, 8)
+    send(0, grads.at[pl.ds(other_half, 512)], pair_in.at[pl.ds(0, 512)], sibling)
+    send(0, grads.at[small], pair_in.at[pl.ds(512, 8)], sibling)
     received(0, pair_in)
-
-    small = grad_ref[1024:1032, :] + pair_in[512:520, :]
-    for step in range(1, 17):
-        other, target = plane_peer(step)
-        row = pl.multiple_of(other * 32, 32)
-        buffer = plane_in if step == 16 else plane_out
-        buffer[other, 0:32, :] = grad_ref[pl.ds(half + row, 32), :] + pair_in[pl.ds(row, 32), :]
-        buffer[other, 32:40, :] = small
-        if step < 16:
-            send(1, plane_out.at[other], plane_in.at[q], target)
-    received(1, plane_in.at[pl.ds(0, 15)])
-    value = plane_in[0]
-    for i in range(1, 16):
-        value = value + plane_in[i]
-    plane_sum[...] = value
-
-    for step in range(1, 5):
-        other, target = z_peer(step)
-        buffer = z_in if step == 4 else z_out
-        buffer[other, 0:8, :] = plane_sum[pl.ds(pl.multiple_of(other * 8, 8), 8), :]
-        buffer[other, 8:16, :] = plane_sum[32:40, :]
-        if step < 4:
-            send(2, z_out.at[other], z_in.at[z], target)
-    received(2, z_in.at[pl.ds(0, 3)])
-    value = (z_in[0] + z_in[1]) + (z_in[2] + z_in[3])
-
-    lot = half + q * 32
-    mine = pl.ds(pl.multiple_of(lot + z * 8, 8), 8)
-    whole[mine, :] = value[0:8]
-    for step in range(1, 4):
-        send(3, whole.at[mine], whole.at[mine], z_peer(step)[1])
-    received(3, whole.at[pl.ds(0, 24)])
-    mine = pl.ds(pl.multiple_of(lot, 32), 32)
-    for step in range(1, 16):
-        send(4, whole.at[mine], whole.at[mine], plane_peer(step)[1])
-    received(4, whole.at[pl.ds(0, 480)])
-    mine = pl.ds(pl.multiple_of(half, 512), 512)
-    send(5, whole.at[mine], whole.at[mine], sibling)
-    whole[1024:1032, :] = value[8:16]
-    received(5, whole.at[pl.ds(0, 512)])
-
-    sent = (
-        pair_in, plane_in.at[pl.ds(0, 15)], z_in.at[pl.ds(0, 3)],
-        whole.at[pl.ds(0, 24)], whole.at[pl.ds(0, 480)], whole.at[pl.ds(0, 512)],
-    )
-    for stage, ref in enumerate(sent):
-        pltpu.make_async_copy(ref, ref, send_sem.at[stage]).wait()
-
-
-def sum_grads(grads):
+    pair_in[0:512, :] += grads[pl.ds(half, 512), :]
+    pair_in[512:520, :] += grads[1024:1032, :]
+
+    def lot(other):
+        return pl.ds(pl.multiple_of(other * 8, 8), 8)
+
+    first = (core == 0) & (number == 0)
+    feeds_first = (core == 0) & (number != 0)
+
+    @pl.when(feeds_first)
+    def _():
+        send(4, pair_in.at[pl.ds(512, 8)], small_in.at[number], device_at({"x": 0, "y": 0, "z": 0}, core))
+
+    @pl.loop(1, 64)
+    def _(step):
+        other, target = peer(step)
+        send(1, pair_in.at[lot(other)], lots_in.at[number], target)
+
+    lots_in[number] = pair_in[lot(number), :]
+    received(1, lots_in.at[pl.ds(0, 63)])
+    mine = pl.ds(pl.multiple_of(half + number * 8, 8), 8)
+    whole[mine, :] = jnp.sum(lots_in[...], axis=0)
+
+    @pl.loop(1, 64)
+    def _(step):
+        send(2, whole.at[mine], whole.at[mine], peer(step)[1])
+
+    @pl.when(first)
+    def _():
+        small_in[0] = pair_in[512:520, :]
+        received(4, small_in.at[pl.ds(0, 63)])
+        whole[1024:1032, :] = jnp.sum(small_in[...], axis=0)
+
+        @pl.loop(1, 64)
+        def _(step):
+            send(5, whole.at[small], whole.at[small], peer(step)[1])
+
+    received(2, whole.at[pl.ds(0, 504)])
+    matrix = pl.ds(pl.multiple_of(half, 512), 512)
+    send(3, whole.at[matrix], whole.at[matrix], sibling)
+
+    @pl.when(feeds_first)
+    def _():
+        received(5, whole.at[small])
+
+    @pl.when(core == 0)
+    def _():
+        send(6, whole.at[small], whole.at[small], sibling)
+
+    @pl.when(core == 1)
+    def _():
+        received(6, whole.at[small])
+
+    received(3, whole.at[pl.ds(0, 512)])
+    sent(0, pair_in)
+    sent(1, lots_in.at[pl.ds(0, 63)])
+    sent(2, whole.at[pl.ds(0, 504)])
+    sent(3, whole.at[pl.ds(0, 512)])
+
+    @pl.when(feeds_first)
+    def _():
+        sent(4, small_in.at[0])
+
+    @pl.when(first)
+    def _():
+        sent(5, small_in.at[pl.ds(0, 63)])
+
+    @pl.when(core == 0)
+    def _():
+        sent(6, whole.at[small])
+
+
+def layer(loss_scale, total, scales, local, w_neigh, head, labels):
     vmem = pl.BlockSpec(memory_space=pltpu.VMEM)
     dma = pltpu.SemaphoreType.DMA
+    width = w_neigh.shape[0]
     return pl.pallas_call(
-        sum_kernel,
+        functools.partial(layer_kernel, loss_scale),
         out_shape=pltpu.VMEM((1032, 128), F32),
-        in_specs=[vmem],
+        in_specs=[vmem] * 6,
         out_specs=vmem,
         scratch_shapes=[
+            pltpu.VMEM((3 * width, width), BF16),
+            pltpu.VMEM((width, width), F32),
+            pltpu.VMEM((width, width), F32),
+            pltpu.VMEM((8, width), F32),
+            pltpu.VMEM((1032, 128), F32),
             pltpu.VMEM((520, 128), F32),
-            pltpu.VMEM((16, 40, 128), F32),
-            pltpu.VMEM((16, 40, 128), F32),
-            pltpu.VMEM((40, 128), F32),
-            pltpu.VMEM((4, 16, 128), F32),
-            pltpu.VMEM((4, 16, 128), F32),
-            dma((6,)),
-            dma((6,)),
+            pltpu.VMEM((64, 8, 128), F32),
+            pltpu.VMEM((64, 8, 128), F32),
+            dma((7,)),
+            dma((7,)),
         ],
         compiler_params=pltpu.CompilerParams(
-            collective_id=1, has_side_effects=True, vmem_limit_bytes=8 * 2**20
+            collective_id=1, has_side_effects=True, vmem_limit_bytes=LAYER_VMEM * 2**20
         ),
-        name="sum_grads",
-    )(grads)
+        name="layer",
+    )(total, scales, local, w_neigh, head, labels)
 
 
 def unpack_kernel(whole, self_ref, neigh_ref, bias_ref, head_ref):
@@ -650,11 +681,8 @@
         hub_block, send_rows, send_count, features.reshape(blocks, 128, width), tile_weights,
         w_self, bias.reshape(1, width),
     )
-    grads = layer(
-        loss_scale, tile_dst, tile_src, tile_count, table, local, weights, sums,
-        w_neigh, w_head.reshape(1, width), labels.reshape(blocks, 128),
-    )
-    return unpack(sum_grads(grads))
+    total, scales = add_tiles(tile_dst, tile_src, tile_count, table, local, weights, sums, blocks)
+    return unpack(layer(loss_scale, total, scales, local, w_neigh, w_head.reshape(1, width), labels.reshape(blocks, 128)))
 
 
 def solution(mesh):

time: 126 us -> 115 us (0.913)
  Pallas kernels: 120 us -> 110 us
    pallas_call x1, Pallas kernels: 31.8 us -> 8.18 us  [add_tiles(): pl.pallas_call(tiles_kernel, out_shape=(pltpu.VMEM((blocks + 1, 128, 256)...]
    pallas_call x1, Pallas kernels: 25.4 us -> 38.4 us  [layer(): pl.pallas_call(functools.partial(layer_kernel, loss_scale), out_shape=plt...]
where the time goes in v5:
time: 115 us
  Pallas kernels  110 us (96%)
  local copies, waits for them, and re-layouts  3.09 us (3%)
  between operations  2.05 us (2%)
    pallas_call x1, Pallas kernels, gather(): pl.pallas_call(gather_kernel, out_shape=(jax.ShapeDtypeStruct((2, 4, 4, 4...  62.4 us
    pallas_call x1, Pallas kernels, layer(): pl.pallas_call(functools.partial(layer_kernel, loss_scale), out_shape=plt...  38.4 us
    pallas_call x1, Pallas kernels, add_tiles(): pl.pallas_call(tiles_kernel, out_shape=(pltpu.VMEM((blocks + 1, 128, 256)...  8.18 us
    unnamed x17, local copies, waits for them, and re-layouts  3.09 us

profile of v5, /device:TPU:1, one launch (start us, length us, event | category | flops | bytes accessed | tf_op | source)
XLA Modules:
  0.0 115.0 jit_solution(4126739473371514511)
XLA Ops:
  0.6 0.0 copy-start.3
  0.6 0.0 copy-start.7
  2.0 0.8 copy.17.rows_ref
  2.8 0.0 copy-start.1
  2.8 0.9 copy-done.1
  3.7 0.0 copy-start.5
  3.7 0.7 copy-done.5
  4.4 0.0 copy-start.6
  4.4 0.7 copy-done.6
  5.0 62.4 %gather.1 = (f32[2,4,4,4,256,128]{5,4,3,2,1,0:T(8,128)}, f32[72,256,128]{2,1,0:T(8,128)S(1)}, bf16[128,128,256]{2,1,0:T(8,128)(2,1)S(1)}, f32[128,128]{1,0:T(8,128)S(1)}) custom-call(s32[1]{0:T(128)S(6)} %copy.19.hub_block_ref, s32[1,128,8]{2,1,0:T(8,128)S(1)} %copy.17.rows_ref, s32[1,128]{1,0:T(1,128)S(1)} %copy-done.6, f32[32,128,256]{2,1,0:T(8,128)} %bitcast.9, ...), custom_call_target="tpu_custom_call" | custom-call | tf_op jit(solution)/shard_map/gather/pallas_call | solution.py:314
  67.5 0.0 copy-done.3
  67.5 0.0 copy-done.7
  67.5 0.0 copy-start
  67.5 0.0 copy-start.2
  67.5 0.0 copy-start.4
  67.5 8.2 %add_tiles.1 = (f32[33,128,256]{2,1,0:T(8,128)S(1)}, f32[128,32]{1,0:T(8,128)S(1)}) custom-call(s32[128]{0:T(128)S(1)} %copy-done.3, s32[128]{0:T(128)S(1)} %copy-done.7, s32[1]{0:T(128)S(6)} %copy.18.count_ref, f32[2,4,4,4,256,128]{5,4,3,2,1,0:T(8,128)} %get-tuple-element.10.table_hbm, f32[72,256,128]{2,1,0:T(8,128)S(1)} %get-tuple-element.11.local_ref, ...), custom_call_target="tpu_custom_call" | custom-call | tf_op jit(solution)/shard_map/add_tiles/pallas_call | solution.py:427
  75.7 0.0 copy-done
  75.7 0.0 copy-done.2
  75.7 0.0 copy-done.4
  75.7 38.4 %layer.1.whole = f32[1032,128]{1,0:T(8,128)S(1)} custom-call(f32[33,128,256]{2,1,0:T(8,128)S(1)} %get-tuple-element.14.total, f32[128,32]{1,0:T(8,128)S(1)} %get-tuple-element.15.scales_ref, f32[72,256,128]{2,1,0:T(8,128)S(1)} %get-tuple-element.11.local_ref, f32[256,256]{1,0:T(8,128)S(1)} %copy-done, f32[1,256]{1,0:T(1,128)S(1)} %bitcast.7, ...), custom_call_target="tpu_custom_call" | custom-call | tf_op jit(solution)/shard_map/layer/pallas_call | solution.py:611
  114.2 0.8 unpack.1
Async XLA Ops:
  0.6 66.8 %copy-start.3 = (s32[128]{0:T(128)S(1)}, s32[128]{0:T(128)}, u32[]{:S(2)}) copy-start(s32[128]{0:T(128)} %dst_ref.1) | copy-start | bytes 1540
  0.6 66.8 %copy-start.7 = (s32[128]{0:T(128)S(1)}, s32[128]{0:T(128)}, u32[]{:S(2)}) copy-start(s32[128]{0:T(128)} %src_ref.1) | copy-start | bytes 1540
  2.8 0.9 copy-start.1
  3.7 0.7 copy-start.5
  4.4 0.7 copy-start.6
  67.5 8.2 %copy-start = (f32[256,256]{1,0:T(8,128)S(1)}, f32[256,256]{1,0:T(8,128)}, u32[]{:S(2)}) copy-start(f32[256,256]{1,0:T(8,128)} %w_neigh_ref.1) | copy-start | bytes 786436
  67.5 8.2 %copy-start.2 = (s32[4096]{0:T(1024)S(1)}, s32[4096]{0:T(1024)}, u32[]{:S(2)}) copy-start(s32[4096]{0:T(1024)} %param.25) | copy-start | bytes 49156
  67.5 8.2 %copy-start.4 = (f32[256]{0:T(256)S(1)}, f32[256]{0:T(256)}, u32[]{:S(2)}) copy-start(f32[256]{0:T(256)} %param.17) | copy-start | bytes 3076

commit v6 on v5

--- a/solution.py
+++ b/solution.py
@@ -58,9 +58,9 @@
 
 
 def gather_kernel(
-    hub_block_ref, rows_ref, count_ref, feat_hbm, weights_hbm, w_self_ref, bias_ref,
+    hub_block_ref, rows_hbm, count_hbm, feat_hbm, weights_hbm, self_hbm, bias_hbm,
     table_ref, local_ref, split_ref, sums_ref,
-    hub, self_k, ring, outbox, inbox,
+    rows_ref, count_ref, w_self_ref, bias_ref, small_sem, hub, self_k, ring, outbox, inbox,
     own_sem, feat_sem, ring_sem, recv1, recv2, recv3, send1, send2, send3, pair_send, pair_recv,
     border_send, border_recv,
 ):
@@ -77,6 +77,12 @@
         number = lax.rem(me + step, 128)
         return number, (lax.div(number, 2), lax.rem(number, 2))
 
+    small_loads = [
+        pltpu.make_async_copy(src, dst, small_sem.at[i])
+        for i, (src, dst) in enumerate((
+            (rows_hbm, rows_ref), (count_hbm, count_ref), (self_hbm, w_self_ref), (bias_hbm, bias_ref),
+        ))
+    ]
     loads = []
     for side in range(2):
         load = pltpu.make_async_copy(
@@ -93,6 +99,8 @@
             weights_hbm.at[pl.ds(i * TILE_CHUNK, TILE_CHUNK)], ring.at[spot], ring_sem.at[spot]
         )
 
+    for load in small_loads:
+        load.start()
     for i in range(TILE_SLOTS):
         load_tiles(i).start()
 
@@ -106,6 +114,8 @@
     for load in loads:
         load.wait()
     hub[...] = local_ref[hub_block_ref[0]]
+    for load in small_loads:
+        load.wait()
     own = pltpu.make_async_copy(hub, table_ref.at[core, z, y, x], own_sem)
     own.start()
     pl.semaphore_wait(barrier, 127)
@@ -156,7 +166,7 @@
             number, target = other(step)
             alive = slot_row < count_ref[0, number]
             for k in range(8):
-                row = rows_ref[0, number, k]
+                row = rows_ref[k, number]
                 block = lax.shift_right_logical(row, 7)
                 inside = row & 127
                 for side in range(2):
@@ -310,7 +320,9 @@
     smem = pl.BlockSpec(memory_space=pltpu.SMEM)
     vmem = pl.BlockSpec(memory_space=pltpu.VMEM)
     hbm = pl.BlockSpec(memory_space=pl.ANY)
+    far = pl.BlockSpec(memory_space=pltpu.HBM)
     border = pltpu.VMEM((128, 2, 8, 128), F32)
+    pin = functools.partial(pltpu.with_memory_space_constraint, memory_space=pltpu.HBM)
     return pl.pallas_call(
         gather_kernel,
         out_shape=(
@@ -319,9 +331,14 @@
             pltpu.VMEM((128, 128, 256), BF16),
             pltpu.VMEM((128, 128), F32),
         ),
-        in_specs=[smem] * 3 + [hbm] * 2 + [vmem] * 2,
+        in_specs=[smem] + [far] * 2 + [hbm] * 2 + [far] * 2,
         out_specs=(hbm,) + (vmem,) * 3,
         scratch_shapes=[
+            pltpu.SMEM(send_rows.shape, jnp.int32),
+            pltpu.SMEM(send_count.shape, jnp.int32),
+            pltpu.VMEM(w_self.shape, F32),
+            pltpu.VMEM(bias.shape, F32),
+            dma((4,)),
             pltpu.VMEM((256, 128), F32),
             pltpu.VMEM((768, 256), BF16),
             pltpu.VMEM((TILE_SLOTS, TILE_CHUNK, 128, 128), F32),
@@ -334,7 +351,7 @@
             collective_id=0, has_side_effects=True, vmem_limit_bytes=GATHER_VMEM * 2**20
         ),
         name="gather",
-    )(hub_block, send_rows, send_count, features, weights, w_self, bias)
+    )(hub_block, pin(send_rows), pin(send_count), features, weights, pin(w_self), pin(bias))
 
 
 GROUP = 4
@@ -437,7 +454,7 @@
     )(dst, src, count, table, local, weights, sums, dst.reshape(1, -1))
 
 
-LAYER_CHUNK = 512
+LAYER_CHUNK = 1024
 
 
 def layer_kernel(
@@ -555,9 +572,15 @@
     mine = pl.ds(pl.multiple_of(half + number * 8, 8), 8)
     whole[mine, :] = jnp.sum(lots_in[...], axis=0)
 
+    def from_plane(z):
+        return recv_sem.at[7 + z]
+
     @pl.loop(1, 64)
     def _(step):
-        send(2, whole.at[mine], whole.at[mine], peer(step)[1])
+        pltpu.make_async_remote_copy(
+            src_ref=whole.at[mine], dst_ref=whole.at[mine], send_sem=send_sem.at[2],
+            recv_sem=from_plane(place["z"]), device_id=peer(step)[1], device_id_type=MESH,
+        ).start()
 
     @pl.when(first)
     def _():
@@ -569,9 +592,12 @@
         def _(step):
             send(5, whole.at[small], whole.at[small], peer(step)[1])
 
-    received(2, whole.at[pl.ds(0, 504)])
-    matrix = pl.ds(pl.multiple_of(half, 512), 512)
-    send(3, whole.at[matrix], whole.at[matrix], sibling)
+    for step in (0, 1, 3, 2):
+        z = lax.rem(place["z"] + step, 4)
+        amount = whole.at[pl.ds(0, 128 if step else 120)]
+        pltpu.make_async_copy(amount, amount, from_plane(z)).wait()
+        plane = pl.ds(pl.multiple_of(half + z * 128, 128), 128)
+        send(3, whole.at[plane], whole.at[plane], sibling)
 
     @pl.when(feeds_first)
     def _():
@@ -623,7 +649,7 @@
             pltpu.VMEM((64, 8, 128), F32),
             pltpu.VMEM((64, 8, 128), F32),
             dma((7,)),
-            dma((7,)),
+            dma((11,)),
         ],
         compiler_params=pltpu.CompilerParams(
             collective_id=1, has_side_effects=True, vmem_limit_bytes=LAYER_VMEM * 2**20
@@ -678,7 +704,7 @@
     vertex_total = features.shape[0] * lax.axis_size(("vert", "row"))
     loss_scale = 1.0 / math.sqrt(vertex_total)
     table, local, weights, sums = gather(
-        hub_block, send_rows, send_count, features.reshape(blocks, 128, width), tile_weights,
+        hub_block, send_rows[0].T, send_count, features.reshape(blocks, 128, width), tile_weights,
         w_self, bias.reshape(1, width),
     )
     total, scales = add_tiles(tile_dst, tile_src, tile_count, table, local, weights, sums, blocks)

time: 115 us -> 106 us (0.922)
  Pallas kernels: 110 us -> 104 us
  local copies, waits for them, and re-layouts: 3.09 us -> 0.03 us
    pallas_call x1, Pallas kernels: 38.4 us -> 35.1 us  [layer(): pl.pallas_call(functools.partial(layer_kernel, loss_scale), out_shape=plt...]
    unnamed x17 -> x10, local copies, waits for them, and re-layouts: 3.09 us -> 0.03 us
    pallas_call x1, Pallas kernels: 62.4 us -> 60.9 us  [gather(): pl.pallas_call(gather_kernel, out_shape=(jax.ShapeDtypeStruct((2, 4, 4, 4...]
where the time goes in v6:
time: 106 us
  Pallas kernels  104 us (98%)
  between operations  2.05 us (2%)
    pallas_call x1, Pallas kernels, gather(): pl.pallas_call(gather_kernel, out_shape=(jax.ShapeDtypeStruct((2, 4, 4, 4...  60.9 us
    pallas_call x1, Pallas kernels, layer(): pl.pallas_call(functools.partial(layer_kernel, loss_scale), out_shape=plt...  35.1 us
    pallas_call x1, Pallas kernels, add_tiles(): pl.pallas_call(tiles_kernel, out_shape=(pltpu.VMEM((blocks + 1, 128, 256)...  7.13 us

profile of v6, /device:TPU:1, one launch (start us, length us, event | category | flops | bytes accessed | tf_op | source)
XLA Modules:
  0.0 106.1 jit_solution(13868660755264085806)
XLA Ops:
  0.6 0.0 copy-start.2
  0.6 0.0 copy-start.4
  2.0 60.9 %gather.1 = (f32[2,4,4,4,256,128]{5,4,3,2,1,0:T(8,128)}, f32[72,256,128]{2,1,0:T(8,128)S(1)}, bf16[128,128,256]{2,1,0:T(8,128)(2,1)S(1)}, f32[128,128]{1,0:T(8,128)S(1)}) custom-call(s32[1]{0:T(128)S(6)} %copy.18.hub_block_ref, s32[8,128]{1,0:T(8,128)} %bitcast.12, s32[1,128]{1,0:T(1,128)} %count_hbm.1, f32[32,128,256]{2,1,0:T(8,128)} %bitcast.11, ...), custom_call_target="tpu_custom_call" | custom-call | tf_op jit(solution)/shard_map/gather/pallas_call | solution.py:326
  62.9 0.0 copy-done.2
  62.9 0.0 copy-done.4
  62.9 0.0 copy-start
  62.9 0.0 copy-start.1
  62.9 0.0 copy-start.3
  62.9 7.1 %add_tiles.1 = (f32[33,128,256]{2,1,0:T(8,128)S(1)}, f32[128,32]{1,0:T(8,128)S(1)}) custom-call(s32[128]{0:T(128)S(1)} %copy-done.2, s32[128]{0:T(128)S(1)} %copy-done.4, s32[1]{0:T(128)S(6)} %copy.17.count_ref, f32[2,4,4,4,256,128]{5,4,3,2,1,0:T(8,128)} %get-tuple-element.10.table_hbm, f32[72,256,128]{2,1,0:T(8,128)S(1)} %get-tuple-element.11.local_ref, ...), custom_call_target="tpu_custom_call" | custom-call | tf_op jit(solution)/shard_map/add_tiles/pallas_call | solution.py:444
  70.1 0.0 copy-done
  70.1 0.0 copy-done.1
  70.1 0.0 copy-done.3
  70.1 35.1 %layer.1.whole = f32[1032,128]{1,0:T(8,128)S(1)} custom-call(f32[33,128,256]{2,1,0:T(8,128)S(1)} %get-tuple-element.14.total, f32[128,32]{1,0:T(8,128)S(1)} %get-tuple-element.15.scales_ref, f32[72,256,128]{2,1,0:T(8,128)S(1)} %get-tuple-element.11.local_ref, f32[256,256]{1,0:T(8,128)S(1)} %copy-done, f32[1,256]{1,0:T(1,128)S(1)} %bitcast.10, ...), custom_call_target="tpu_custom_call" | custom-call | tf_op jit(solution)/shard_map/layer/pallas_call | solution.py:637
  105.2 0.8 unpack.1
Async XLA Ops:
  0.6 62.3 %copy-start.2 = (s32[128]{0:T(128)S(1)}, s32[128]{0:T(128)}, u32[]{:S(2)}) copy-start(s32[128]{0:T(128)} %dst_ref.1) | copy-start | bytes 1540
  0.6 62.3 %copy-start.4 = (s32[128]{0:T(128)S(1)}, s32[128]{0:T(128)}, u32[]{:S(2)}) copy-start(s32[128]{0:T(128)} %src_ref.1) | copy-start | bytes 1540
  62.9 7.2 %copy-start = (f32[256,256]{1,0:T(8,128)S(1)}, f32[256,256]{1,0:T(8,128)}, u32[]{:S(2)}) copy-start(f32[256,256]{1,0:T(8,128)} %w_neigh_ref.1) | copy-start | bytes 786436
  62.9 7.2 %copy-start.1 = (s32[4096]{0:T(1024)S(1)}, s32[4096]{0:T(1024)}, u32[]{:S(2)}) copy-start(s32[4096]{0:T(1024)} %param.25) | copy-start | bytes 49156
  62.9 7.2 %copy-start.3 = (f32[256]{0:T(256)S(1)}, f32[256]{0:T(256)}, u32[]{:S(2)}) copy-start(f32[256]{0:T(256)} %param.17) | copy-start | bytes 3076

commit v7 on v6

--- a/solution.py
+++ b/solution.py
@@ -51,7 +51,7 @@
     return lax.dot_general(a, b, dims, preferred_element_type=F32)
 
 
-GATHER_VMEM, TILES_VMEM, LAYER_VMEM = 34, 30, 30
+GATHER_VMEM, TILES_VMEM, LAYER_VMEM = 20, 12, 20
 CHUNK = 256
 TILE_CHUNK = 8
 TILE_SLOTS = 4
@@ -326,13 +326,13 @@
     return pl.pallas_call(
         gather_kernel,
         out_shape=(
-            jax.ShapeDtypeStruct((2, 4, 4, 4, 256, 128), F32),
+            pltpu.VMEM((2, 4, 4, 4, 256, 128), F32),
             pltpu.VMEM((72, 256, 128), F32),
             pltpu.VMEM((128, 128, 256), BF16),
             pltpu.VMEM((128, 128), F32),
         ),
         in_specs=[smem] + [far] * 2 + [hbm] * 2 + [far] * 2,
-        out_specs=(hbm,) + (vmem,) * 3,
+        out_specs=(vmem,) * 4,
         scratch_shapes=[
             pltpu.SMEM(send_rows.shape, jnp.int32),
             pltpu.SMEM(send_count.shape, jnp.int32),
@@ -359,33 +359,24 @@
 
 def tiles_kernel(
     dst_ref, src_ref, count_ref,
-    table_hbm, local_ref, split_ref, sums_ref, dst_row_ref,
+    table_ref, local_ref, split_ref, sums_ref, dst_row_ref,
     total, scales_ref,
-    table_ref, near_tiles, low_tiles, high_tiles, table_sem,
+    near_tiles, hub_tiles,
 ):
     tiles = split_ref.shape[0]
     blocks = total.shape[0] - 1
     first_hub = blocks + 8
     count = count_ref[0]
 
-    table_loads = [
-        pltpu.make_async_copy(table_hbm.at[i // 4, i % 4], table_ref.at[i // 4, i % 4], table_sem.at[i])
-        for i in range(8)
-    ]
-    for load in table_loads:
-        load.start()
     total[...] = jnp.zeros_like(total)
 
     def sort_tile(tile, ends):
-        src = src_ref[tile]
-        near = jnp.where(src < first_hub, 1, 0)
-        high = (1 - near) * (lax.shift_right_logical(src - first_hub, 1) & 1)
-        kinds = (near, 1 - near - high, high)
-        for listed, end in zip((near_tiles, low_tiles, high_tiles), ends):
+        near = jnp.where(src_ref[tile] < first_hub, 1, 0)
+        for listed, end in zip((near_tiles, hub_tiles), ends):
             listed[end] = tile
-        return tuple(end + kind for end, kind in zip(ends, kinds))
-
-    amounts = lax.fori_loop(0, count, sort_tile, (0, 0, 0))
+        return ends[0] + near, ends[1] + (1 - near)
+
+    amounts = lax.fori_loop(0, count, sort_tile, (0, 0))
 
     def wide(block):
         return jnp.concatenate([block[0:128], block[128:256]], axis=1)
@@ -413,11 +404,8 @@
         1.0 + (dot(sums_high, chosen, by_lanes) + dot(sums_low, chosen, by_lanes) + dot(sums_rest, chosen, by_lanes))
     )
 
-    work = ((near_tiles, near_source, ()), (low_tiles, hub_source, table_loads[:4]), (high_tiles, hub_source, table_loads[4:]))
-    for (listed, source, loads), amount in zip(work, amounts):
-        for load in loads:
-            load.wait()
-
+    work = ((near_tiles, near_source), (hub_tiles, hub_source))
+    for (listed, source), amount in zip(work, amounts):
         @pl.loop(0, lax.div(amount + (GROUP - 1), GROUP))
         def _(group):
             products, targets = [], []
@@ -444,14 +432,14 @@
     return pl.pallas_call(
         tiles_kernel,
         out_shape=(pltpu.VMEM((blocks + 1, 128, 256), F32), pltpu.VMEM((128, blocks), F32)),
-        in_specs=[smem] * 3 + [pl.BlockSpec(memory_space=pl.ANY)] + [vmem] * 4,
+        in_specs=[smem] * 3 + [vmem] * 5,
         out_specs=(vmem, vmem),
         scratch_shapes=[
-            pltpu.VMEM(table.shape, F32), listed, listed, listed, pltpu.SemaphoreType.DMA((8,)),
+            listed, listed,
         ],
         compiler_params=pltpu.CompilerParams(vmem_limit_bytes=TILES_VMEM * 2**20),
         name="add_tiles",
-    )(dst, src, count, table, local, weights, sums, dst.reshape(1, -1))
+    )(dst, src, count, *(pltpu.with_memory_space_constraint(v, pltpu.VMEM) for v in (table, local, weights)), sums, dst.reshape(1, -1))
 
 
 LAYER_CHUNK = 1024

time: 106 us -> 105 us (level)
  no operation moved by 1% of the time
where the time goes in v7:
time: 105 us
  Pallas kernels  103 us (98%)
  between operations  2.05 us (2%)
    pallas_call x1, Pallas kernels, gather(): pl.pallas_call(gather_kernel, out_shape=(pltpu.VMEM((2, 4, 4, 4, 256, 128...  60.1 us
    pallas_call x1, Pallas kernels, layer(): pl.pallas_call(functools.partial(layer_kernel, loss_scale), out_shape=plt...  35 us
    pallas_call x1, Pallas kernels, add_tiles(): pl.pallas_call(tiles_kernel, out_shape=(pltpu.VMEM((blocks + 1, 128, 256)...  7.05 us

profile of v7, /device:TPU:1, one launch (start us, length us, event | category | flops | bytes accessed | tf_op | source)
XLA Modules:
  0.0 105.0 jit_solution(9768425679170723264)
XLA Ops:
  0.6 0.0 copy-start.2
  0.6 0.0 copy-start.4
  2.0 60.1 %gather.1 = (f32[2,4,4,4,256,128]{5,4,3,2,1,0:T(8,128)S(1)}, f32[72,256,128]{2,1,0:T(8,128)S(1)}, bf16[128,128,256]{2,1,0:T(8,128)(2,1)S(1)}, f32[128,128]{1,0:T(8,128)S(1)}) custom-call(s32[1]{0:T(128)S(6)} %copy.18.hub_block_ref, s32[8,128]{1,0:T(8,128)} %bitcast.12, s32[1,128]{1,0:T(1,128)} %count_hbm.1, f32[32,128,256]{2,1,0:T(8,128)} %bitcast.11, ...), custom_call_target="tpu_custom_call" | custom-call | tf_op jit(solution)/shard_map/gather/pallas_call | solution.py:326
  62.1 0.0 copy-done.2
  62.1 0.0 copy-done.4
  62.1 0.0 copy-start
  62.1 0.0 copy-start.1
  62.1 0.0 copy-start.3
  62.1 7.0 %add_tiles.1 = (f32[33,128,256]{2,1,0:T(8,128)S(1)}, f32[128,32]{1,0:T(8,128)S(1)}) custom-call(s32[128]{0:T(128)S(1)} %copy-done.2, s32[128]{0:T(128)S(1)} %copy-done.4, s32[1]{0:T(128)S(6)} %copy.17.count_ref, f32[2,4,4,4,256,128]{5,4,3,2,1,0:T(8,128)S(1)} %get-tuple-element.10.table_ref, f32[72,256,128]{2,1,0:T(8,128)S(1)} %get-tuple-element.11.local_ref, ...), custom_call_target="tpu_custom_call" | custom-call | tf_op jit(solution)/shard_map/add_tiles/pallas_call | solution.py:432
  69.2 0.0 copy-done
  69.2 0.0 copy-done.1
  69.2 0.0 copy-done.3
  69.2 35.0 %layer.1.whole = f32[1032,128]{1,0:T(8,128)S(1)} custom-call(f32[33,128,256]{2,1,0:T(8,128)S(1)} %get-tuple-element.14.total, f32[128,32]{1,0:T(8,128)S(1)} %get-tuple-element.15.scales_ref, f32[72,256,128]{2,1,0:T(8,128)S(1)} %get-tuple-element.11.local_ref, f32[256,256]{1,0:T(8,128)S(1)} %copy-done, f32[1,256]{1,0:T(1,128)S(1)} %bitcast.10, ...), custom_call_target="tpu_custom_call" | custom-call | tf_op jit(solution)/shard_map/layer/pallas_call | solution.py:625
  104.2 0.8 unpack.1
Async XLA Ops:
  0.6 61.4 %copy-start.2 = (s32[128]{0:T(128)S(1)}, s32[128]{0:T(128)}, u32[]{:S(2)}) copy-start(s32[128]{0:T(128)} %dst_ref.1) | copy-start | bytes 1540
  0.6 61.4 %copy-start.4 = (s32[128]{0:T(128)S(1)}, s32[128]{0:T(128)}, u32[]{:S(2)}) copy-start(s32[128]{0:T(128)} %src_ref.1) | copy-start | bytes 1540
  62.1 7.1 %copy-start = (f32[256,256]{1,0:T(8,128)S(1)}, f32[256,256]{1,0:T(8,128)}, u32[]{:S(2)}) copy-start(f32[256,256]{1,0:T(8,128)} %w_neigh_ref.1) | copy-start | bytes 786436
  62.1 7.1 %copy-start.1 = (s32[4096]{0:T(1024)S(1)}, s32[4096]{0:T(1024)}, u32[]{:S(2)}) copy-start(s32[4096]{0:T(1024)} %param.25) | copy-start | bytes 49156
  62.1 7.1 %copy-start.3 = (f32[256]{0:T(256)S(1)}, f32[256]{0:T(256)}, u32[]{:S(2)}) copy-start(f32[256]{0:T(256)} %param.17) | copy-start | bytes 3076

commit v8 on v7

--- a/solution.py
+++ b/solution.py
@@ -1,4 +1,5 @@
 import functools
+import itertools
 import math
 
 import jax
@@ -354,7 +355,7 @@
     )(hub_block, pin(send_rows), pin(send_count), features, weights, pin(w_self), pin(bias))
 
 
-GROUP = 4
+GROUP = 16
 
 
 def tiles_kernel(
@@ -442,7 +443,7 @@
     )(dst, src, count, *(pltpu.with_memory_space_constraint(v, pltpu.VMEM) for v in (table, local, weights)), sums, dst.reshape(1, -1))
 
 
-LAYER_CHUNK = 1024
+LAYER_CHUNK = 2048
 
 
 def layer_kernel(
@@ -455,17 +456,23 @@
     number = (place["z"] * 4 + place["y"]) * 4 + place["x"]
     sibling = device_at(place, 1 - core)
 
-    def peer(step):
-        other = lax.rem(number + step, 64)
-        at = {"x": lax.rem(other, 4), "y": lax.rem(lax.div(other, 4), 4), "z": lax.div(other, 16)}
-        return other, device_at(at, core)
+    away = {
+        axis: [lax.rem(place[axis] + step, 4) for step in range(4)] for axis in "xyz"
+    }
+    along_y = [lax.div(y, 2) * 8 + core for y in away["y"]]
+    row_y = [lax.rem(y, 2) for y in away["y"]]
+    peers = []
+    for dz, dy, dx in itertools.product(range(4), repeat=3):
+        if dz + dy + dx:
+            vert = away["z"][dz] * 16 + along_y[dy] + away["x"][dx] * 2
+            other = away["z"][dz] * 16 + away["y"][dy] * 4 + away["x"][dx]
+            peers.append((other, (vert, row_y[dy])))
 
     barrier = pltpu.get_barrier_semaphore()
     pl.semaphore_signal(barrier, inc=1, device_id=sibling, device_id_type=MESH)
 
-    @pl.loop(1, 64)
-    def _(step):
-        pl.semaphore_signal(barrier, inc=1, device_id=peer(step)[1], device_id_type=MESH)
+    for _, target in peers:
+        pl.semaphore_signal(barrier, inc=1, device_id=target, device_id_type=MESH)
 
     blocks = labels_ref.shape[0]
     neigh_high, neigh_low = split(w_neigh_ref[...])
@@ -550,9 +557,7 @@
     def _():
         send(4, pair_in.at[pl.ds(512, 8)], small_in.at[number], device_at({"x": 0, "y": 0, "z": 0}, core))
 
-    @pl.loop(1, 64)
-    def _(step):
-        other, target = peer(step)
+    for other, target in peers:
         send(1, pair_in.at[lot(other)], lots_in.at[number], target)
 
     lots_in[number] = pair_in[lot(number), :]
@@ -563,11 +568,10 @@
     def from_plane(z):
         return recv_sem.at[7 + z]
 
-    @pl.loop(1, 64)
-    def _(step):
+    for _, target in peers:
         pltpu.make_async_remote_copy(
             src_ref=whole.at[mine], dst_ref=whole.at[mine], send_sem=send_sem.at[2],
-            recv_sem=from_plane(place["z"]), device_id=peer(step)[1], device_id_type=MESH,
+            recv_sem=from_plane(place["z"]), device_id=target, device_id_type=MESH,
         ).start()
 
     @pl.when(first)
@@ -576,9 +580,8 @@
         received(4, small_in.at[pl.ds(0, 63)])
         whole[1024:1032, :] = jnp.sum(small_in[...], axis=0)
 
-        @pl.loop(1, 64)
-        def _(step):
-            send(5, whole.at[small], whole.at[small], peer(step)[1])
+        for _, target in peers:
+            send(5, whole.at[small], whole.at[small], target)
 
     for step in (0, 1, 3, 2):
         z = lax.rem(place["z"] + step, 4)

time: 105 us -> 100 us (0.952)
  Pallas kernels: 103 us -> 97.8 us
    pallas_call x1, Pallas kernels: 7.05 us -> 3.57 us  [add_tiles(): pl.pallas_call(tiles_kernel, out_shape=(pltpu.VMEM((blocks + 1, 128, 256)...]
    pallas_call x1, Pallas kernels: 35 us -> 33.3 us  [layer(): pl.pallas_call(functools.partial(layer_kernel, loss_scale), out_shape=plt...]
where the time goes in v8:
time: 100 us; the launch traced here: 99.9 us
  Pallas kernels  97.8 us (98%)
  between operations  2.05 us (2%)
    pallas_call x1, Pallas kernels, gather(): pl.pallas_call(gather_kernel, out_shape=(pltpu.VMEM((2, 4, 4, 4, 256, 128...  60.1 us
    pallas_call x1, Pallas kernels, layer(): pl.pallas_call(functools.partial(layer_kernel, loss_scale), out_shape=plt...  33.3 us
    pallas_call x1, Pallas kernels, add_tiles(): pl.pallas_call(tiles_kernel, out_shape=(pltpu.VMEM((blocks + 1, 128, 256)...  3.57 us

profile of v8, /device:TPU:1, one launch (start us, length us, event | category | flops | bytes accessed | tf_op | source)
XLA Modules:
  0.0 99.9 jit_solution(2210275272083233586)
XLA Ops:
  0.6 0.0 copy-start.2
  0.6 0.0 copy-start.4
  2.0 60.1 %gather.1 = (f32[2,4,4,4,256,128]{5,4,3,2,1,0:T(8,128)S(1)}, f32[72,256,128]{2,1,0:T(8,128)S(1)}, bf16[128,128,256]{2,1,0:T(8,128)(2,1)S(1)}, f32[128,128]{1,0:T(8,128)S(1)}) custom-call(s32[1]{0:T(128)S(6)} %copy.18.hub_block_ref, s32[8,128]{1,0:T(8,128)} %bitcast.12, s32[1,128]{1,0:T(1,128)} %count_hbm.1, f32[32,128,256]{2,1,0:T(8,128)} %bitcast.11, ...), custom_call_target="tpu_custom_call" | custom-call | tf_op jit(solution)/shard_map/gather/pallas_call | solution.py:327
  62.1 0.0 copy-done.2
  62.1 0.0 copy-done.4
  62.1 0.0 copy-start
  62.1 0.0 copy-start.1
  62.1 0.0 copy-start.3
  62.1 3.6 %add_tiles.1 = (f32[33,128,256]{2,1,0:T(8,128)S(1)}, f32[128,32]{1,0:T(8,128)S(1)}) custom-call(s32[128]{0:T(128)S(1)} %copy-done.2, s32[128]{0:T(128)S(1)} %copy-done.4, s32[1]{0:T(128)S(6)} %copy.17.count_ref, f32[2,4,4,4,256,128]{5,4,3,2,1,0:T(8,128)S(1)} %get-tuple-element.10.table_ref, f32[72,256,128]{2,1,0:T(8,128)S(1)} %get-tuple-element.11.local_ref, ...), custom_call_target="tpu_custom_call" | custom-call | tf_op jit(solution)/shard_map/add_tiles/pallas_call | solution.py:433
  65.7 0.0 copy-done
  65.7 0.0 copy-done.1
  65.7 0.0 copy-done.3
  65.7 33.3 %layer.1.whole = f32[1032,128]{1,0:T(8,128)S(1)} custom-call(f32[33,128,256]{2,1,0:T(8,128)S(1)} %get-tuple-element.14.total, f32[128,32]{1,0:T(8,128)S(1)} %get-tuple-element.15.scales_ref, f32[72,256,128]{2,1,0:T(8,128)S(1)} %get-tuple-element.11.local_ref, f32[256,256]{1,0:T(8,128)S(1)} %copy-done, f32[1,256]{1,0:T(1,128)S(1)} %bitcast.10, ...), custom_call_target="tpu_custom_call" | custom-call | tf_op jit(solution)/shard_map/layer/pallas_call | solution.py:628
  99.0 0.8 unpack.1
Async XLA Ops:
  0.6 61.4 %copy-start.2 = (s32[128]{0:T(128)S(1)}, s32[128]{0:T(128)}, u32[]{:S(2)}) copy-start(s32[128]{0:T(128)} %dst_ref.1) | copy-start | bytes 1540
  0.6 61.4 %copy-start.4 = (s32[128]{0:T(128)S(1)}, s32[128]{0:T(128)}, u32[]{:S(2)}) copy-start(s32[128]{0:T(128)} %src_ref.1) | copy-start | bytes 1540
  62.1 3.6 %copy-start = (f32[256,256]{1,0:T(8,128)S(1)}, f32[256,256]{1,0:T(8,128)}, u32[]{:S(2)}) copy-start(f32[256,256]{1,0:T(8,128)} %w_neigh_ref.1) | copy-start | bytes 786436
  62.1 3.6 %copy-start.1 = (s32[4096]{0:T(1024)S(1)}, s32[4096]{0:T(1024)}, u32[]{:S(2)}) copy-start(s32[4096]{0:T(1024)} %param.25) | copy-start | bytes 49156
  62.1 3.6 %copy-start.3 = (f32[256]{0:T(256)S(1)}, f32[256]{0:T(256)}, u32[]{:S(2)}) copy-start(f32[256]{0:T(256)} %param.17) | copy-start | bytes 3076

commit v9 on v8

--- a/solution.py
+++ b/solution.py
@@ -63,13 +63,13 @@
     table_ref, local_ref, split_ref, sums_ref,
     rows_ref, count_ref, w_self_ref, bias_ref, small_sem, hub, self_k, ring, outbox, inbox,
     own_sem, feat_sem, ring_sem, recv1, recv2, recv3, send1, send2, send3, pair_send, pair_recv,
-    border_send, border_recv,
+    border_send, border_recv, ready,
 ):
     place, core = my_place()
     x, y, z = place["x"], place["y"], place["z"]
     near = {}
     for axis in "xyz":
-        for step in (1, 3):
+        for step in (1, 2, 3):
             near[axis, step] = device_at(shifted(place, axis, step), core)
     sibling = device_at(place, 1 - core)
     me = lax.axis_index("vert") * 2 + lax.axis_index("row")
@@ -106,10 +106,9 @@
         load_tiles(i).start()
 
     barrier = pltpu.get_barrier_semaphore()
-
-    @pl.loop(1, 128)
-    def _(step):
-        pl.semaphore_signal(barrier, inc=1, device_id=other(step)[1], device_id_type=MESH)
+    close = list(near.values()) + [sibling]
+    for target in close:
+        pl.semaphore_signal(barrier, inc=1, device_id=target, device_id_type=MESH)
 
 
     for load in loads:
@@ -119,7 +118,16 @@
         load.wait()
     own = pltpu.make_async_copy(hub, table_ref.at[core, z, y, x], own_sem)
     own.start()
-    pl.semaphore_wait(barrier, 127)
+    pl.semaphore_wait(barrier, len(close))
+
+    def tell(n):
+        for target in close:
+            pl.semaphore_signal(ready.at[n], inc=1, device_id=target, device_id_type=MESH)
+
+    def hear(n):
+        pl.semaphore_wait(ready.at[n], len(close))
+
+    tell(0)
 
     def slot(part, where, half=None):
         start, rows = PART_START[part], PART_ROWS[part]
@@ -231,7 +239,6 @@
         send_both(p, {}, second, send2.at[p], recv2.at[p, 0])
 
     sums_ref[...] = jnp.zeros_like(sums_ref)
-    border_go(1, 65)
     own.wait()
     for side, offset in ((0, 3), (1, 1)):
         unit = OFFSETS.index(offset)
@@ -241,8 +248,11 @@
             arrived(p, where, first, recv1.at[p, side])
             pass_on(p, where, first, send1.at[p], recv1.at[p], side)
             send_both(p, where, second, send2.at[p], recv2.at[p, unit])
-    border_go(65, 128)
-    border_go(128, 129)
+        if side == 0:
+            hear(0)
+            tell(1)
+    hear(1)
+    tell(2)
     for p in parts:
         first, second, third = PART_AXES[p]
         where = {first: 2}
@@ -257,6 +267,8 @@
     self_k[256:512, :] = self_high
     self_k[512:768, :] = self_low
 
+    hear(2)
+    border_go(1, 65)
     for unit in range(4):
         for side, offset in ((0, 3), (1, 1)):
             for p in parts:
@@ -270,6 +282,8 @@
             line = {first: "all", second: offset}
             send_both(p, line, third, send3.at[p], recv3.at[p, 1 + side])
             to_sibling(p, line)
+    border_go(65, 128)
+    border_go(128, 129)
     for p in parts:
         first, second, third = PART_AXES[p]
         for unit in range(4):
@@ -346,7 +360,7 @@
             border, border,
             dma, dma((2,)), dma((TILE_SLOTS,)), dma((3, 4)), dma((3, 4, 4)), dma((3, 4, 4)),
             dma((3,)), dma((3,)), dma((3,)), dma, dma,
-            dma, dma,
+            dma, dma, pltpu.SemaphoreType.REGULAR((3,)),
         ],
         compiler_params=pltpu.CompilerParams(
             collective_id=0, has_side_effects=True, vmem_limit_bytes=GATHER_VMEM * 2**20

time: 100 us -> 95.5 us (0.955)
  Pallas kernels: 97.8 us -> 93.3 us
    pallas_call x1, Pallas kernels: 33.3 us -> 31 us  [layer(): pl.pallas_call(functools.partial(layer_kernel, loss_scale), out_shape=plt...]
    pallas_call x1, Pallas kernels: 60.1 us -> 57.9 us  [gather(): pl.pallas_call(gather_kernel, out_shape=(pltpu.VMEM((2, 4, 4, 4, 256, 128...]
where the time goes in v9:
time: 95.5 us; the launch traced here: 95.3 us
  Pallas kernels  93.3 us (98%)
  between operations  2.05 us (2%)
    pallas_call x1, Pallas kernels, gather(): pl.pallas_call(gather_kernel, out_shape=(pltpu.VMEM((2, 4, 4, 4, 256, 128...  57.9 us
    pallas_call x1, Pallas kernels, layer(): pl.pallas_call(functools.partial(layer_kernel, loss_scale), out_shape=plt...  31 us
    pallas_call x1, Pallas kernels, add_tiles(): pl.pallas_call(tiles_kernel, out_shape=(pltpu.VMEM((blocks + 1, 128, 256)...  3.57 us

profile of v9, /device:TPU:1, one launch (start us, length us, event | category | flops | bytes accessed | tf_op | source)
XLA Modules:
  0.0 95.3 jit_solution(9183613242454715873)
XLA Ops:
  0.6 0.0 copy-start.2
  0.6 0.0 copy-start.4
  2.0 57.9 %gather.1 = (f32[2,4,4,4,256,128]{5,4,3,2,1,0:T(8,128)S(1)}, f32[72,256,128]{2,1,0:T(8,128)S(1)}, bf16[128,128,256]{2,1,0:T(8,128)(2,1)S(1)}, f32[128,128]{1,0:T(8,128)S(1)}) custom-call(s32[1]{0:T(128)S(6)} %copy.18.hub_block_ref, s32[8,128]{1,0:T(8,128)} %bitcast.12, s32[1,128]{1,0:T(1,128)} %count_hbm.1, f32[32,128,256]{2,1,0:T(8,128)} %bitcast.11, ...), custom_call_target="tpu_custom_call" | custom-call | tf_op jit(solution)/shard_map/gather/pallas_call | solution.py:341
  59.8 0.0 copy-done.2
  59.9 0.0 copy-done.4
  59.9 0.0 copy-start
  59.9 0.0 copy-start.1
  59.9 0.0 copy-start.3
  59.9 3.6 %add_tiles.1 = (f32[33,128,256]{2,1,0:T(8,128)S(1)}, f32[128,32]{1,0:T(8,128)S(1)}) custom-call(s32[128]{0:T(128)S(1)} %copy-done.2, s32[128]{0:T(128)S(1)} %copy-done.4, s32[1]{0:T(128)S(6)} %copy.17.count_ref, f32[2,4,4,4,256,128]{5,4,3,2,1,0:T(8,128)S(1)} %get-tuple-element.10.table_ref, f32[72,256,128]{2,1,0:T(8,128)S(1)} %get-tuple-element.11.local_ref, ...), custom_call_target="tpu_custom_call" | custom-call | tf_op jit(solution)/shard_map/add_tiles/pallas_call | solution.py:447
  63.5 0.0 copy-done
  63.5 0.0 copy-done.1
  63.5 0.0 copy-done.3
  63.5 31.0 %layer.1.whole = f32[1032,128]{1,0:T(8,128)S(1)} custom-call(f32[33,128,256]{2,1,0:T(8,128)S(1)} %get-tuple-element.14.total, f32[128,32]{1,0:T(8,128)S(1)} %get-tuple-element.15.scales_ref, f32[72,256,128]{2,1,0:T(8,128)S(1)} %get-tuple-element.11.local_ref, f32[256,256]{1,0:T(8,128)S(1)} %copy-done, f32[1,256]{1,0:T(1,128)S(1)} %bitcast.10, ...), custom_call_target="tpu_custom_call" | custom-call | tf_op jit(solution)/shard_map/layer/pallas_call | solution.py:642
  94.5 0.8 unpack.1
Async XLA Ops:
  0.6 59.2 %copy-start.2 = (s32[128]{0:T(128)S(1)}, s32[128]{0:T(128)}, u32[]{:S(2)}) copy-start(s32[128]{0:T(128)} %dst_ref.1) | copy-start | bytes 1540
  0.6 59.2 %copy-start.4 = (s32[128]{0:T(128)S(1)}, s32[128]{0:T(128)}, u32[]{:S(2)}) copy-start(s32[128]{0:T(128)} %src_ref.1) | copy-start | bytes 1540
  59.9 3.6 %copy-start = (f32[256,256]{1,0:T(8,128)S(1)}, f32[256,256]{1,0:T(8,128)}, u32[]{:S(2)}) copy-start(f32[256,256]{1,0:T(8,128)} %w_neigh_ref.1) | copy-start | bytes 786436
  59.9 3.6 %copy-start.1 = (s32[4096]{0:T(1024)S(1)}, s32[4096]{0:T(1024)}, u32[]{:S(2)}) copy-start(s32[4096]{0:T(1024)} %param.25) | copy-start | bytes 49156
  59.9 3.6 %copy-start.3 = (f32[256]{0:T(256)S(1)}, f32[256]{0:T(256)}, u32[]{:S(2)}) copy-start(f32[256]{0:T(256)} %param.17) | copy-start | bytes 3076

commit v10 on v9

--- a/solution.py
+++ b/solution.py
@@ -386,12 +386,13 @@
     total[...] = jnp.zeros_like(total)
 
     def sort_tile(tile, ends):
-        near = jnp.where(src_ref[tile] < first_hub, 1, 0)
+        used = jnp.where(tile < count, 1, 0)
+        near = jnp.where(src_ref[tile] < first_hub, used, 0)
         for listed, end in zip((near_tiles, hub_tiles), ends):
             listed[end] = tile
-        return ends[0] + near, ends[1] + (1 - near)
-
-    amounts = lax.fori_loop(0, count, sort_tile, (0, 0))
+        return ends[0] + near, ends[1] + (used - near)
+
+    amounts = lax.fori_loop(0, tiles, sort_tile, (0, 0), unroll=8)
 
     def wide(block):
         return jnp.concatenate([block[0:128], block[128:256]], axis=1)

time: 95.5 us -> 94.9 us (level)
    pallas_call x1, Pallas kernels: 31 us -> 25.8 us  [layer(): pl.pallas_call(functools.partial(layer_kernel, loss_scale), out_shape=plt...]
    pallas_call x1, Pallas kernels: 3.57 us -> 8.59 us  [add_tiles(): pl.pallas_call(tiles_kernel, out_shape=(pltpu.VMEM((blocks + 1, 128, 256)...]
where the time goes in v10:
time: 94.9 us; the launch traced here: 95.2 us
  Pallas kernels  93.1 us (98%)
  between operations  2.05 us (2%)
    pallas_call x1, Pallas kernels, gather(): pl.pallas_call(gather_kernel, out_shape=(pltpu.VMEM((2, 4, 4, 4, 256, 128...  57.9 us
    pallas_call x1, Pallas kernels, layer(): pl.pallas_call(functools.partial(layer_kernel, loss_scale), out_shape=plt...  25.8 us
    pallas_call x1, Pallas kernels, add_tiles(): pl.pallas_call(tiles_kernel, out_shape=(pltpu.VMEM((blocks + 1, 128, 256)...  8.59 us

profile of v10, /device:TPU:1, one launch (start us, length us, event | category | flops | bytes accessed | tf_op | source)
XLA Modules:
  0.0 95.2 jit_solution(12325871411002355796)
XLA Ops:
  0.6 0.0 copy-start.2
  0.6 0.0 copy-start.4
  2.0 57.9 %gather.1 = (f32[2,4,4,4,256,128]{5,4,3,2,1,0:T(8,128)S(1)}, f32[72,256,128]{2,1,0:T(8,128)S(1)}, bf16[128,128,256]{2,1,0:T(8,128)(2,1)S(1)}, f32[128,128]{1,0:T(8,128)S(1)}) custom-call(s32[1]{0:T(128)S(6)} %copy.18.hub_block_ref, s32[8,128]{1,0:T(8,128)} %bitcast.12, s32[1,128]{1,0:T(1,128)} %count_hbm.1, f32[32,128,256]{2,1,0:T(8,128)} %bitcast.11, ...), custom_call_target="tpu_custom_call" | custom-call | tf_op jit(solution)/shard_map/gather/pallas_call | solution.py:341
  59.8 0.0 copy-done.2
  59.9 0.0 copy-done.4
  59.9 0.0 copy-start
  59.9 0.0 copy-start.1
  59.9 0.0 copy-start.3
  59.9 8.6 %add_tiles.1 = (f32[33,128,256]{2,1,0:T(8,128)S(1)}, f32[128,32]{1,0:T(8,128)S(1)}) custom-call(s32[128]{0:T(128)S(1)} %copy-done.2, s32[128]{0:T(128)S(1)} %copy-done.4, s32[1]{0:T(128)S(6)} %copy.17.count_ref, f32[2,4,4,4,256,128]{5,4,3,2,1,0:T(8,128)S(1)} %get-tuple-element.10.table_ref, f32[72,256,128]{2,1,0:T(8,128)S(1)} %get-tuple-element.11.local_ref, ...), custom_call_target="tpu_custom_call" | custom-call | tf_op jit(solution)/shard_map/add_tiles/pallas_call | solution.py:448
  68.5 0.0 copy-done
  68.5 0.0 copy-done.1
  68.5 0.0 copy-done.3
  68.5 25.8 %layer.1.whole = f32[1032,128]{1,0:T(8,128)S(1)} custom-call(f32[33,128,256]{2,1,0:T(8,128)S(1)} %get-tuple-element.14.total, f32[128,32]{1,0:T(8,128)S(1)} %get-tuple-element.15.scales_ref, f32[72,256,128]{2,1,0:T(8,128)S(1)} %get-tuple-element.11.local_ref, f32[256,256]{1,0:T(8,128)S(1)} %copy-done, f32[1,256]{1,0:T(1,128)S(1)} %bitcast.10, ...), custom_call_target="tpu_custom_call" | custom-call | tf_op jit(solution)/shard_map/layer/pallas_call | solution.py:643
  94.4 0.8 unpack.1
Async XLA Ops:
  0.6 59.2 %copy-start.2 = (s32[128]{0:T(128)S(1)}, s32[128]{0:T(128)}, u32[]{:S(2)}) copy-start(s32[128]{0:T(128)} %dst_ref.1) | copy-start | bytes 1540
  0.6 59.2 %copy-start.4 = (s32[128]{0:T(128)S(1)}, s32[128]{0:T(128)}, u32[]{:S(2)}) copy-start(s32[128]{0:T(128)} %src_ref.1) | copy-start | bytes 1540
  59.9 8.6 %copy-start = (f32[256,256]{1,0:T(8,128)S(1)}, f32[256,256]{1,0:T(8,128)}, u32[]{:S(2)}) copy-start(f32[256,256]{1,0:T(8,128)} %w_neigh_ref.1) | copy-start | bytes 786436
  59.9 8.6 %copy-start.1 = (s32[4096]{0:T(1024)S(1)}, s32[4096]{0:T(1024)}, u32[]{:S(2)}) copy-start(s32[4096]{0:T(1024)} %param.25) | copy-start | bytes 49156
  59.9 8.6 %copy-start.3 = (f32[256]{0:T(256)S(1)}, f32[256]{0:T(256)}, u32[]{:S(2)}) copy-start(f32[256]{0:T(256)} %param.17) | copy-start | bytes 3076
